TPU v7x, 32 devices: a whole 2x2x4 slice. The times are simulated.
32 devices in a mesh: dp: 8 (over z, y), feat: 4 (over x, core).
Axes of the slice: x: 2, y: 2, z: 4, core: 2. Of those that a mesh axis runs over, the one named last changes fastest.
Arguments:
- observations: bfloat16 [1024, 128, 128], P('dp', 'feat'), may hold values from -1.5 to 1.5
- labels: int32 [1024, 128], P('dp'), may hold values 0 or 1
- tile_live: int32 [1024], P('dp'), may hold values from 1 to 128
- tile_group: int32 [1024], P('dp'), may hold values from 0 to 127, as said below
- position: float32 [128, 2048], P('dp', 'feat'), may hold values from -2.4 to 2.4
- momentum: float32 [128, 2048], P('dp', 'feat'), may hold values from -6 to 6
- gradient: float32 [128, 2048], P('dp', 'feat'), may hold values from -18 to 18
- prior_mean: float32 [2048], P('feat'), may hold values from -1.8 to 1.8
- prior_prec: float32 [128], P('feat'), may hold values from 0.25 to 4
- inv_mass: float32 [128], P('feat'), may hold values from 0.5 to 2
Outputs:
- new_position: float32 [128, 2048], P('dp', 'feat')
- new_momentum: float32 [128, 2048], P('dp', 'feat')
- new_gradient: float32 [128, 2048], P('dp', 'feat')
- energy: float32 [128, 16], P('dp')
Inputs may be any that keep to these rules, and one draw needn't show every extreme that they name: `tile_group`: group g belongs to owner g // 16. Among the 128 tiles of one device at most 32 have groups of any one owner, and one owner has exactly 32 tiles from every device. `tile_live`: the live slots of a tile come first.
All inputs are finite; a program needn't handle non-finite values. No bound on the sum of `labels` on one device may be relied on, other than what follows from the above.
Results may differ from a plain program's by a relative error of at most 0.0041.
Values may be sent and summed in bfloat16 or wider, within the bound.
No kernel may reach another device: no remote copies, remote signals or barrier semaphores. Data moves between devices by JAX's collectives and lax.ppermute only.
A program may use at most 64 MiB of HBM per device.

v0:
```python
import jax
import jax.numpy as jnp
from jax import lax
from jax.sharding import PartitionSpec as P

step_size = 0.1


def likelihood(logits, labels, tile_live):
    row_count = logits.shape[2]
    live_rows = (jnp.arange(row_count, dtype=jnp.int32)[None, :] < tile_live[:, None])[:, None, :]
    targets = labels.astype(jnp.float32)[:, None, :]
    residual = jnp.where(live_rows, jax.nn.sigmoid(logits) - targets, 0.0).astype(jnp.bfloat16)
    neg_loglik = jnp.sum(
        jnp.where(live_rows, jax.nn.softplus(logits) - targets * logits, 0.0), axis=2
    )
    return (residual, neg_loglik)


def body(
    observations,
    labels,
    tile_live,
    tile_group,
    position,
    momentum,
    gradient,
    prior_mean,
    prior_prec,
    inv_mass,
):
    owners = lax.axis_size("dp")
    owner_index = lax.axis_index("dp")
    tile_count, quarter, row_count = observations.shape
    own_groups = position.shape[0]
    block_width = position.shape[1]
    chains = block_width // quarter
    slot_count = max(2, 2 * tile_count // owners)
    prior_full = jnp.repeat(prior_prec, chains)
    mass_full = jnp.repeat(inv_mass, chains)
    half_momentum = momentum - 0.5 * step_size * gradient
    moved_position = position + step_size * mass_full * half_momentum
    rounded = moved_position.astype(jnp.bfloat16)
    target = tile_group // own_groups
    tile_order = jnp.arange(tile_count, dtype=jnp.int32)
    earlier = (target[:, None] == target[None, :]) & (tile_order[None, :] < tile_order[:, None])
    slot_rank = jnp.sum(earlier.astype(jnp.int32), axis=1)
    slot_place = target * slot_count + slot_rank
    slot_tile = jnp.full((owners * slot_count,), -1, jnp.int32).at[slot_place].set(tile_order)
    filled = slot_tile >= 0
    safe_tile = jnp.maximum(slot_tile, 0)
    requests = jnp.where(filled, tile_group[safe_tile], -1).reshape(owners, slot_count)
    group_order = jnp.arange(own_groups, dtype=jnp.int32)
    asked_groups = lax.all_to_all(requests, "dp", split_axis=0, concat_axis=0, tiled=True)
    local_group = asked_groups - owner_index * own_groups
    selector = (local_group[:, :, None] == group_order[None, None, :]).astype(jnp.bfloat16)
    picked = jnp.einsum(
        "nkg,gw->nkw", selector, rounded, preferred_element_type=jnp.float32
    ).astype(jnp.bfloat16)
    fetched = lax.all_to_all(picked, "dp", split_axis=0, concat_axis=0, tiled=True)
    tile_blocks = fetched.reshape(owners * slot_count, block_width)[slot_place]
    tile_coeffs = tile_blocks.reshape(tile_count, quarter, chains)
    partial_logits = jnp.einsum(
        "tfc,tfr->tcr", tile_coeffs, observations, preferred_element_type=jnp.float32
    )
    logit_share = lax.psum_scatter(partial_logits, "feat", scatter_dimension=0, tiled=True)
    share_count = logit_share.shape[0]
    share_start = lax.axis_index("feat") * share_count
    share_labels = lax.dynamic_slice_in_dim(labels, share_start, share_count, 0)
    share_live = lax.dynamic_slice_in_dim(tile_live, share_start, share_count, 0)
    residual_share, loglik_share = likelihood(logit_share, share_labels, share_live)
    residual = lax.all_gather(residual_share, "feat", axis=0, tiled=True)
    neg_loglik = lax.dynamic_update_slice_in_dim(
        jnp.zeros((tile_count, chains), jnp.float32), loglik_share, share_start, 0
    )
    partial_grad = jnp.einsum(
        "tfr,tcr->tfc", observations, residual, preferred_element_type=jnp.float32
    ).reshape(tile_count, block_width)
    send_grad = jnp.where(filled[:, None], partial_grad[safe_tile], 0.0).reshape(
        owners, slot_count, block_width
    )
    send_loglik = jnp.where(filled[:, None], neg_loglik[safe_tile], 0.0).reshape(
        owners, slot_count, chains
    )
    got_grad, got_loglik = (
        lax.all_to_all(send_grad, "dp", split_axis=0, concat_axis=0, tiled=True),
        lax.all_to_all(send_loglik, "dp", split_axis=0, concat_axis=0, tiled=True),
    )
    local_slot = asked_groups.reshape(-1) - owner_index * own_groups
    collector = (group_order[:, None] == local_slot[None, :]).astype(jnp.float32)
    likelihood_grad = jnp.dot(
        collector,
        got_grad.reshape(-1, block_width),
        precision=lax.Precision.HIGHEST,
        preferred_element_type=jnp.float32,
    )
    group_loglik = jnp.dot(
        collector,
        got_loglik.reshape(-1, chains),
        precision=lax.Precision.HIGHEST,
        preferred_element_type=jnp.float32,
    )
    offset = moved_position - prior_mean
    new_gradient = likelihood_grad + prior_full * offset
    new_momentum = half_momentum - 0.5 * step_size * new_gradient
    quadratic = 0.5 * (prior_full * offset * offset + mass_full * new_momentum * new_momentum)
    quadratic = jnp.sum(quadratic.reshape(own_groups, quarter, chains), axis=1)
    summed = quadratic + group_loglik
    energy = lax.psum(summed, "feat")
    return (moved_position, new_momentum, new_gradient, energy)


def solution(mesh):
    placed = (
        P("dp", "feat", None),
        P("dp", None),
        P("dp"),
        P("dp"),
        P("dp", "feat"),
        P("dp", "feat"),
        P("dp", "feat"),
        P("feat"),
        P("feat"),
        P("feat"),
    )
    return jax.shard_map(
        body,
        mesh=mesh,
        in_specs=placed,
        out_specs=(P("dp", "feat"), P("dp", "feat"), P("dp", "feat"), P("dp", None)),
        check_vma=False,
    )
```

profile of v0, /device:TPU:0, one launch (start us, length us, event | category | flops | bytes accessed | tf_op | source)
XLA Modules:
  0.0 121.5 jit_solution(3610660603039455534)
XLA Ops:
  7.2 0.8 and_select_fusion
  7.9 0.2 convert_reduce_fusion
  8.1 0.5 copy-done.1
  8.6 1.0 scatter_custom_fusion
  9.7 1.9 %gather_fusion = s32[256]{0:T(256)S(1)} fusion(s32[128]{0:T(128)S(1)} %copy-done.1, s32[1024]{0:T(1024)S(1)} %pad_clamp_fusion.1), kind=kCustom, calls=%fused_computation | custom fusion | bytes 3072 | tf_op jit(solution)/shard_map/gather | solution.py:52
  11.6 0.7 all_to_all.15
  12.2 7.3 %all-to-all-start = ((s32[8,1,32]{2,1,0:T(1,128)}), s32[8,1,32]{2,1,0:T(1,128)S(1)}, u32[]{:S(2)}, u32[]{:S(2)}) async-start(s32[8,1,32]{2,1,0:T(1,128)} %all_to_all.15), calls=%async_computation | async-start | bytes 8192 | tf_op jit(solution)/shard_map/all_to_all | solution.py:54
  19.6 0.1 reshape.91
  19.8 6.2 %all-to-all-done = s32[8,1,32]{2,1,0:T(1,128)S(1)} async-done(((s32[8,1,32]{2,1,0:T(1,128)}), s32[8,1,32]{2,1,0:T(1,128)S(1)}, u32[]{:S(2)}, u32[]{:S(2)}) %all-to-all-start) | async-done | bytes 1056 | tf_op jit(solution)/shard_map/all_to_all | solution.py:54
  26.0 0.5 broadcast.89
  26.5 0.7 fusion.13
  27.1 1.0 convolution_convert_fusion
  28.1 3.4 %all-to-all-start.1 = ((bf16[8,32,512]{2,1,0:T(8,128)(2,1)}), bf16[8,32,512]{2,1,0:T(8,128)(2,1)S(1)}, u32[]{:S(2)}, u32[]{:S(2)}) async-start(bf16[8,32,512]{2,1,0:T(8,128)(2,1)} %convolution_convert_fusion), calls=%async_computation.1 | async-start | bytes 524288 | tf_op jit(solution)/shard_map/all_to_all | solution.py:60
  31.6 8.1 %all-to-all-done.1 = bf16[8,32,512]{2,1,0:T(8,128)(2,1)S(1)} async-done(((bf16[8,32,512]{2,1,0:T(8,128)(2,1)}), bf16[8,32,512]{2,1,0:T(8,128)(2,1)S(1)}, u32[]{:S(2)}, u32[]{:S(2)}) %all-to-all-start.1) | async-done | bytes 262176 | tf_op jit(solution)/shard_map/all_to_all | solution.py:60
  39.7 0.8 gather_fusion.1
  40.5 0.1 copy.30
  40.7 0.5 copy.31
  41.1 1.4 %fusion.15 = f32[128,16,128]{2,1,0:T(8,128)} fusion(bf16[128,32,16]{1,2,0:T(8,128)(2,1)S(1)} %copy.31, bf16[128,32,128]{2,1,0:T(8,128)(2,1)S(1)} %copy-done), kind=kOutput, calls=%fused_computation.52 | convolution fusion | flops 16777216 | bytes 2228224 | tf_op jit(solution)/shard_map/tfc,tfr->tcr/dot_general | solution.py:63
  42.6 0.1 broadcast_in_dim.85
  42.6 0.7 copy-done.9
  43.3 0.1 dynamic_slice.6
  43.4 0.7 dynamic-slice_convert_fusion
  44.1 0.1 iota_compare_fusion.3
  44.2 21.8 %reduce-scatter.2.cloned.1.call-done = f32[32,16,128]{2,1,0:T(8,128)} async-done(((f32[128,16,128]{2,1,0:T(8,128)}), f32[32,16,128]{2,1,0:T(8,128)}) %reduce-scatter.2.cloned.1.call-update) | async-done | bytes 262160 | tf_op jit(solution)/shard_map/reduce_scatter | solution.py:66
  66.0 1.3 %fusion.2 = (f32[32,16]{1,0:T(8,128)S(1)}, bf16[32,16,128]{2,1,0:T(8,128)(2,1)S(1)}) fusion(f32[32,16,128]{2,1,0:T(8,128)} %reduce-scatter.2.cloned.1.call-done, f32[32,128]{1,0:T(8,128)S(1)} %dynamic-slice_convert_fusion, pred[32,128]{1,0:T(8,128)(4,1)S(1)} %iota_compare_fusion.3), kind=kLoop, calls=%fused_computation.12 | loop fusion | flops 1048064 | bytes 415744 | tf_op jit(solution)/shard_map/reduce_sum | solution.py:14
  67.2 6.6 %all_gather.3 = bf16[128,16,128]{2,1,0:T(8,128)(2,1)S(1)} all-gather(bf16[32,16,128]{2,1,0:T(8,128)(2,1)S(1)} %get-tuple-element.11), channel_id=1, replica_groups=mesh['dp'=8,'feat'=4] {'feat'}, dimensions={0}, use_global_device_ids=true | all-gather | bytes 655360 | tf_op jit(solution)/shard_map/all_gather | solution.py:72
  73.8 0.7 convolution_bitcast_fusion
  74.5 0.5 copy.32
  75.0 0.1 copy.33
  75.1 1.0 gather_fusion.2
  76.1 0.7 gather_fusion.3
  76.9 0.1 copy.34
  77.0 0.7 reshape.155
  77.7 5.5 %all-to-all-start.3 = ((f32[8,1,512]{2,1,0:T(1,128)}), f32[8,1,512]{2,1,0:T(1,128)S(1)}, u32[]{:S(2)}, u32[]{:S(2)}) async-start(f32[8,1,512]{2,1,0:T(1,128)} %reshape.155), calls=%async_computation.4 | async-start | bytes 32768 | tf_op jit(solution)/shard_map/all_to_all | solution.py:87
  83.2 0.9 broadcast_select_fusion
  84.1 5.7 %all-to-all-done.3 = f32[8,1,512]{2,1,0:T(1,128)S(1)} async-done(((f32[8,1,512]{2,1,0:T(1,128)}), f32[8,1,512]{2,1,0:T(1,128)S(1)}, u32[]{:S(2)}, u32[]{:S(2)}) %all-to-all-start.3) | async-done | bytes 16416 | tf_op jit(solution)/shard_map/all_to_all | solution.py:87
  89.8 3.5 %all-to-all-start.2 = ((f32[8,32,512]{2,1,0:T(8,128)}), f32[8,32,512]{2,1,0:T(8,128)S(1)}, u32[]{:S(2)}, u32[]{:S(2)}) async-start(f32[8,32,512]{2,1,0:T(8,128)} %broadcast_select_fusion), calls=%async_computation.3 | async-start | bytes 1048576 | tf_op jit(solution)/shard_map/all_to_all | solution.py:86
  93.3 0.1 mul.86
  93.4 0.1 sub.57
  93.5 0.5 broadcast.94
  94.0 0.7 reduce.5
  94.7 0.1 reshape.156
  94.8 0.1 reshape.97
  94.9 12.2 %all-to-all-done.2 = f32[8,32,512]{2,1,0:T(8,128)S(1)} async-done(((f32[8,32,512]{2,1,0:T(8,128)}), f32[8,32,512]{2,1,0:T(8,128)S(1)}, u32[]{:S(2)}, u32[]{:S(2)}) %all-to-all-start.2) | async-done | bytes 524320 | tf_op jit(solution)/shard_map/all_to_all | solution.py:86
  107.1 0.9 fusion.5
  108.0 0.1 reshape.96
  108.2 0.1 convolution_add_fusion.1
  108.3 6.3 %psum.7 = f32[16,16]{1,0:T(8,128)} all-reduce(f32[16,16]{1,0:T(8,128)S(1)} %convolution_add_fusion.1), channel_id=1, replica_groups=mesh['dp'=8,'feat'=4] {'feat'}, use_global_device_ids=true, to_apply=%region_5.6 | all-reduce | flops 256 | bytes 2048 | tf_op jit(solution)/shard_map/psum | solution.py:109
  (35 shorter events, 0.4 us)
Async XLA Ops:
  7.2 34.0 %copy-start = (bf16[128,32,128]{2,1,0:T(8,128)(2,1)S(1)}, bf16[128,32,128]{2,1,0:T(8,128)(2,1)}, u32[]{:S(2)}) copy-start(bf16[128,32,128]{2,1,0:T(8,128)(2,1)} %param.10) | copy-start | bytes 3145732
  7.9 0.7 copy-start.1
  9.6 9.9 %copy-start.7 = (f32[32]{0:T(128)S(1)}, f32[32]{0:T(128)}, u32[]{:S(2)}) copy-start(f32[32]{0:T(128)} %param.19) | copy-start | bytes 388
  9.6 10.1 %copy-start.4 = (f32[16,512]{1,0:T(8,128)S(1)}, f32[16,512]{1,0:T(8,128)}, u32[]{:S(2)}) copy-start(f32[16,512]{1,0:T(8,128)} %param.16) | copy-start | bytes 98308
  9.6 10.1 %copy-start.5 = (f32[16,512]{1,0:T(8,128)S(1)}, f32[16,512]{1,0:T(8,128)}, u32[]{:S(2)}) copy-start(f32[16,512]{1,0:T(8,128)} %param.14) | copy-start | bytes 98308
  11.5 8.2 %copy-start.3 = (f32[16,512]{1,0:T(8,128)S(1)}, f32[16,512]{1,0:T(8,128)}, u32[]{:S(2)}) copy-start(f32[16,512]{1,0:T(8,128)} %param.15) | copy-start | bytes 98308
  12.2 13.7 %all-to-all-start = ((s32[8,1,32]{2,1,0:T(1,128)}), s32[8,1,32]{2,1,0:T(1,128)S(1)}, u32[]{:S(2)}, u32[]{:S(2)}) async-start(s32[8,1,32]{2,1,0:T(1,128)} %all_to_all.15), calls=%async_computation | async-start | bytes 8192 | tf_op jit(solution)/shard_map/all_to_all | solution.py:54
  19.8 87.3 %copy-start.2 = (f32[16,512]{1,0:T(8,128)}, f32[16,512]{1,0:T(8,128)S(1)}, u32[]{:S(2)}) copy-start(f32[16,512]{1,0:T(8,128)S(1)} %multiply_add_fusion) | copy-start | bytes 98308
  28.1 11.6 %all-to-all-start.1 = ((bf16[8,32,512]{2,1,0:T(8,128)(2,1)}), bf16[8,32,512]{2,1,0:T(8,128)(2,1)S(1)}, u32[]{:S(2)}, u32[]{:S(2)}) async-start(bf16[8,32,512]{2,1,0:T(8,128)(2,1)} %convolution_convert_fusion), calls=%async_computation.1 | async-start | bytes 524288 | tf_op jit(solution)/shard_map/all_to_all | solution.py:60
  31.5 34.5 %reduce-scatter.2.cloned.1.call-start = ((), (), s32[]{:S(2)}) async-start(), calls=%async_computation.5 | async-start | bytes 1310720 | tf_op jit(solution)/shard_map/reduce_scatter | solution.py:66
  42.6 0.7 copy-start.9
  77.7 12.1 %all-to-all-start.3 = ((f32[8,1,512]{2,1,0:T(1,128)}), f32[8,1,512]{2,1,0:T(1,128)S(1)}, u32[]{:S(2)}, u32[]{:S(2)}) async-start(f32[8,1,512]{2,1,0:T(1,128)} %reshape.155), calls=%async_computation.4 | async-start | bytes 32768 | tf_op jit(solution)/shard_map/all_to_all | solution.py:87
  84.1 9.2 %copy-start.8 = (f32[32]{0:T(128)S(1)}, f32[32]{0:T(128)}, u32[]{:S(2)}) copy-start(f32[32]{0:T(128)} %param.18) | copy-start | bytes 388
  89.8 17.3 %all-to-all-start.2 = ((f32[8,32,512]{2,1,0:T(8,128)}), f32[8,32,512]{2,1,0:T(8,128)S(1)}, u32[]{:S(2)}, u32[]{:S(2)}) async-start(f32[8,32,512]{2,1,0:T(8,128)} %broadcast_select_fusion), calls=%async_computation.3 | async-start | bytes 1048576 | tf_op jit(solution)/shard_map/all_to_all | solution.py:86
  94.8 12.3 %copy-start.6 = (f32[512]{0:T(512)S(1)}, f32[512]{0:T(512)}, u32[]{:S(2)}) copy-start(f32[512]{0:T(512)} %param.17) | copy-start | bytes 6148
Sparse Core Ops, SparseCore 0:
  42.7 23.2 reduce-scatter.1
where the time goes:
time: 122 us; the launch traced here: 121 us
  waiting for transfers between devices  54 us (44%)
  starting transfers between devices  19.8 us (16%)
  between operations  14.3 us (12%)
  blocking collectives  12.9 us (11%)
  local copies, waits for them, and re-layouts  11.1 us (9%)
  other arithmetic  5.32 us (4%)
  matrix products  4.04 us (3%)
    reduce_scatter x1, waiting for transfers between devices, body(): lax.psum_scatter(partial_logits, 'feat', scatter_dimension=0, tiled=True)  21.8 us
    all_to_all x1, waiting for transfers between devices, body(): lax.all_to_all(send_grad, 'dp', split_axis=0, concat_axis=0, tiled=True)  12.2 us
    all_to_all x1, waiting for transfers between devices, body(): lax.all_to_all(picked, 'dp', split_axis=0, concat_axis=0, tiled=True)  8.1 us
    all_to_all x1, starting transfers between devices, body(): lax.all_to_all(requests, 'dp', split_axis=0, concat_axis=0, tiled=True)  7.31 us
    all_gather x1, blocking collectives, body(): residual = lax.all_gather(residual_share, 'feat', axis=0, tiled=True)  6.59 us
    psum x1, blocking collectives, body(): energy = lax.psum(summed, 'feat')  6.34 us
    all_to_all x1, waiting for transfers between devices, body(): lax.all_to_all(requests, 'dp', split_axis=0, concat_axis=0, tiled=True)  6.19 us
    all_to_all x1, waiting for transfers between devices, body(): lax.all_to_all(send_loglik, 'dp', split_axis=0, concat_axis=0, tiled=True)  5.68 us
  transfers between devices with their start and end apart: 5, of which 5 were waited for; matrix products, arithmetic and copies ran while one was open for 3% of the time, Pallas kernels for 0%

commit v1 on v0

v1 whole, which is shorter than its diff:
```python
import jax
import jax.numpy as jnp
from jax import lax
from jax.sharding import PartitionSpec as P

step_size = 0.1


def likelihood(logits, labels, tile_live):
    row_count = logits.shape[2]
    live_rows = (jnp.arange(row_count, dtype=jnp.int32)[None, :] < tile_live[:, None])[:, None, :]
    targets = labels.astype(jnp.float32)[:, None, :]
    residual = jnp.where(live_rows, jax.nn.sigmoid(logits) - targets, 0.0).astype(jnp.bfloat16)
    neg_loglik = jnp.sum(
        jnp.where(live_rows, jax.nn.softplus(logits) - targets * logits, 0.0), axis=2
    )
    return (residual, neg_loglik)


def body(
    observations,
    labels,
    tile_live,
    tile_group,
    position,
    momentum,
    gradient,
    prior_mean,
    prior_prec,
    inv_mass,
):
    owners = lax.axis_size("dp")
    parts = lax.axis_size("feat")
    part_index = lax.axis_index("feat")
    tile_count, quarter, row_count = observations.shape
    own_groups, block_width = position.shape
    chains = block_width // quarter
    groups = owners * own_groups
    share = tile_count // parts

    share_obs = lax.all_to_all(
        observations.reshape(parts, share, quarter, row_count), "feat", 0, 0, tiled=True
    )

    prior_full = jnp.repeat(prior_prec, chains)
    mass_full = jnp.repeat(inv_mass, chains)
    half_momentum = momentum - 0.5 * step_size * gradient
    moved_position = position + step_size * mass_full * half_momentum
    rounded = moved_position.astype(jnp.bfloat16)
    table = lax.all_gather(rounded, ("feat", "dp"), axis=0, tiled=True)
    table = table.reshape(parts, groups, block_width)

    start = part_index * share
    share_labels = lax.dynamic_slice_in_dim(labels, start, share, 0)
    share_live = lax.dynamic_slice_in_dim(tile_live, start, share, 0)
    share_group = lax.dynamic_slice_in_dim(tile_group, start, share, 0)
    member = share_group[:, None] == jnp.arange(groups, dtype=jnp.int32)[None, :]

    coeffs = jnp.einsum(
        "tg,qgw->qtw", member.astype(jnp.bfloat16), table, preferred_element_type=jnp.float32
    ).astype(jnp.bfloat16)
    coeffs = coeffs.reshape(parts, share, quarter, chains)
    logits = jnp.einsum(
        "qtfc,qtfr->tcr", coeffs, share_obs, preferred_element_type=jnp.float32
    )
    residual, neg_loglik = likelihood(logits, share_labels, share_live)
    grad = jnp.einsum(
        "qtfr,tcr->tqfc", share_obs, residual, preferred_element_type=jnp.float32
    ).reshape(share, parts * block_width)
    chooser = member.astype(jnp.float32)
    group_grad = jnp.einsum(
        "tg,tw->gw", chooser, grad, precision=lax.Precision.HIGHEST,
        preferred_element_type=jnp.float32,
    ).astype(jnp.bfloat16)
    group_loglik = jnp.einsum(
        "tg,tc->gc", chooser, neg_loglik, precision=lax.Precision.HIGHEST,
        preferred_element_type=jnp.float32,
    )
    high = group_loglik.astype(jnp.bfloat16)
    low = (group_loglik - high.astype(jnp.float32)).astype(jnp.bfloat16)
    pad = jnp.zeros((groups, parts - 2, chains), jnp.bfloat16)
    tails = jnp.concatenate([high[:, None], low[:, None], pad], axis=1)
    send = jnp.concatenate([group_grad.reshape(groups, parts, block_width), tails], axis=2)
    send = send.reshape(owners, own_groups, parts, block_width + chains).transpose(0, 2, 1, 3)
    send = send.reshape(owners * parts, own_groups, block_width + chains)
    got = lax.all_to_all(send, ("dp", "feat"), 0, 0, tiled=True)
    summed = jnp.sum(got.astype(jnp.float32), axis=0)
    likelihood_grad = summed[:, :block_width]
    own_loglik = summed[:, block_width:]

    offset = moved_position - prior_mean
    new_gradient = likelihood_grad + prior_full * offset
    new_momentum = half_momentum - 0.5 * step_size * new_gradient
    quadratic = 0.5 * (prior_full * offset * offset + mass_full * new_momentum * new_momentum)
    quadratic = jnp.sum(quadratic.reshape(own_groups, quarter, chains), axis=1)
    energy = lax.psum(quadratic + own_loglik, "feat")
    return (moved_position, new_momentum, new_gradient, energy)


def solution(mesh):
    placed = (
        P("dp", "feat", None),
        P("dp", None),
        P("dp"),
        P("dp"),
        P("dp", "feat"),
        P("dp", "feat"),
        P("dp", "feat"),
        P("feat"),
        P("feat"),
        P("feat"),
    )
    return jax.shard_map(
        body,
        mesh=mesh,
        in_specs=placed,
        out_specs=(P("dp", "feat"), P("dp", "feat"), P("dp", "feat"), P("dp", None)),
        check_vma=False,
    )
```

time: 122 us -> 116 us (0.951)
  blocking collectives: 12.9 us -> 80.3 us
  waiting for transfers between devices: 54 us -> 17.8 us
  between operations: 14.3 us -> 0.82 us
  starting transfers between devices: 19.8 us -> 7.13 us
  local copies, waits for them, and re-layouts: 11.1 us -> 3.54 us
  other arithmetic: 5.32 us -> 2.59 us
    all_gather x1, blocking collectives: 6.59 us -> 72.7 us  [body(): table = lax.all_gather(rounded, ('feat', 'dp'), axis=0, tiled=True)]
    reduce_scatter x1 -> x0, waiting for transfers between devices: 21.8 us -> none  [body(): lax.psum_scatter(partial_logits, 'feat', scatter_dimension=0, tiled=True)]
    all_to_all x4 -> x2, waiting for transfers between devices: 32.1 us -> 17.8 us  [the longest x1 17.8 us: body(): got = lax.all_to_all(send, ('dp', 'feat'), 0, 0, tiled=True)]
    all_to_all x4 -> x2, starting transfers between devices: 19.7 us -> 7.13 us  [the longest x1 4.38 us: body(): lax.all_to_all(observations.reshape(parts, share, quarter, row_count), 'f...]
    gather x6 -> x0, local copies, waits for them, and re-layouts: 4.62 us -> none  [the longest x1 1.87 us: body(): tile_group[safe_tile]]
    unnamed x22 -> x18, local copies, waits for them, and re-layouts: 1.97 us -> 0.04 us
    select_n x4 -> x0, other arithmetic: 1.67 us -> none  [the longest x1 0.9 us: body(): jnp.where(filled[:, None], partial_grad[safe_tile], 0.0)]
    reduce_sum x2 -> x1, other arithmetic: 1.43 us -> 0.11 us  [body(): summed = jnp.sum(got.astype(jnp.float32), axis=0)]
  transfers between devices with their start and end apart: 5 -> 2, of which waited for: 5 -> 1; matrix products, arithmetic and copies ran while one was open for 3% -> 2% of each run, Pallas kernels for 0% -> 0%
where the time goes in v1:
time: 116 us; the launch traced here: 115 us
  blocking collectives  80.3 us (69%)
  waiting for transfers between devices  17.8 us (15%)
  starting transfers between devices  7.13 us (6%)
  local copies, waits for them, and re-layouts  3.54 us (3%)
  matrix products  3.27 us (3%)
  other arithmetic  2.59 us (2%)
    all_gather x1, blocking collectives, body(): table = lax.all_gather(rounded, ('feat', 'dp'), axis=0, tiled=True)  72.7 us
    all_to_all x1, waiting for transfers between devices, body(): got = lax.all_to_all(send, ('dp', 'feat'), 0, 0, tiled=True)  17.8 us
    psum x1, blocking collectives, body(): energy = lax.psum(quadratic + own_loglik, 'feat')  7.52 us
    all_to_all x1, starting transfers between devices, body(): lax.all_to_all(observations.reshape(parts, share, quarter, row_count), 'f...  4.38 us
    all_to_all x1, starting transfers between devices, body(): got = lax.all_to_all(send, ('dp', 'feat'), 0, 0, tiled=True)  2.75 us
  transfers between devices with their start and end apart: 2, of which 1 were waited for; matrix products, arithmetic and copies ran while one was open for 2% of the time, Pallas kernels for 0%

profile of v1, /device:TPU:0, one launch (start us, length us, event | category | flops | bytes accessed | tf_op | source)
XLA Modules:
  0.0 115.4 jit_solution(13545249069612451096)
XLA Ops:
  0.6 0.0 copy-start.5
  0.6 0.0 copy-start.7
  0.7 0.0 copy-start
  0.7 0.0 copy-start.1
  0.7 0.0 copy-start.3
  0.7 4.4 %all-to-all-start = ((bf16[4,32,32,128]{3,2,1,0:T(8,128)(2,1)}), bf16[4,32,32,128]{3,2,1,0:T(8,128)(2,1)S(1)}, u32[]{:S(2)}, u32[]{:S(2)}) async-start(bf16[4,32,32,128]{3,2,1,0:T(8,128)(2,1)} %bitcast.31), calls=%async_computation | async-start | bytes 2097152 | tf_op jit(solution)/shard_map/all_to_all | solution.py:41
  5.1 0.0 copy-done.5
  5.1 0.1 broadcast_in_dim.35
  5.1 0.1 reshape.66
  5.2 0.0 copy-done.7
  5.2 0.1 dynamic_slice.9
  5.3 0.0 copy-done
  5.3 0.0 copy-done.1
  5.3 0.0 copy-done.3
  5.3 0.0 copy-start.2
  5.3 72.7 %all_gather.3 = bf16[512,512]{1,0:T(8,128)(2,1)S(1)} all-gather(bf16[16,512]{1,0:T(8,128)(2,1)S(1)} %get-tuple-element.9), channel_id=1, replica_groups=mesh['dp'=8,'feat'=4] {'feat','dp'}, dimensions={0}, use_global_device_ids=true | all-gather | bytes 540672 | tf_op jit(solution)/shard_map/all_gather | solution.py:50
  78.1 0.0 copy-start.8
  78.1 0.2 fusion
  78.3 0.3 copy.24
  78.6 1.0 copy.25
  79.6 0.0 copy-done.8
  79.6 0.1 dynamic_slice.10
  79.7 0.7 dynamic-slice_convert_fusion
  80.4 0.1 iota_compare_fusion
  80.5 0.0 all-to-all-done
  80.5 0.6 fusion.5
  81.1 1.5 %convolution_bitcast_fusion = f32[32,4,32,16]{2,3,1,0:T(8,128)S(1)} fusion(bf16[4,32,32,128]{3,2,1,0:T(8,128)(2,1)S(1)} %all-to-all-done, f32[32,16,128]{2,1,0:T(8,128)S(1)} %get-tuple-element.12, f32[32,128]{1,0:T(8,128)S(1)} %dynamic-slice_convert_fusion, pred[32,128]{1,0:T(8,128)(4,1)S(1)} %iota_compare_fusion), kind=kOutput, calls=%fused_computation.1 | convolution fusion | flops 17170432 | bytes 1593344 | tf_op jit(solution)/shard_map/qtfr,tcr->tqfc/dot_general | solution.py:67
  82.6 0.9 copy.28
  83.5 0.7 convolution_convert_fusion
  84.3 0.4 concatenate.14
  84.6 0.1 copy.31
  84.8 0.2 subtract_convert_fusion
  85.0 0.1 copy.34
  85.1 0.1 copy.35
  85.2 0.0 copy-start.6
  85.2 1.0 maximum_maximum_fusion
  86.2 0.0 copy-start.4
  86.2 2.7 %all-to-all-start.1 = ((bf16[32,16,528]{2,1,0:T(8,128)(2,1)}), bf16[32,16,528]{2,1,0:T(8,128)(2,1)S(1)}, u32[]{:S(2)}, u32[]{:S(2)}) async-start(bf16[32,16,528]{2,1,0:T(8,128)(2,1)} %bitcast.14), calls=%async_computation.1 | async-start | bytes 1310720 | tf_op jit(solution)/shard_map/all_to_all | solution.py:86
  89.0 0.0 copy-done.6
  89.0 0.1 broadcast_in_dim.39
  89.0 0.1 mul.74
  89.1 17.8 %all-to-all-done.1 = bf16[32,16,528]{2,1,0:T(8,128)(2,1)S(1)} async-done(((bf16[32,16,528]{2,1,0:T(8,128)(2,1)}), bf16[32,16,528]{2,1,0:T(8,128)(2,1)S(1)}, u32[]{:S(2)}, u32[]{:S(2)}) %all-to-all-start.1) | async-done | bytes 540704 | tf_op jit(solution)/shard_map/all_to_all | solution.py:86
  107.0 0.1 convert_reduce_fusion
  107.1 0.0 copy-done.2
  107.1 0.0 copy-done.4
  107.1 0.6 fusion.11
  107.7 0.1 reshape.72
  107.9 7.5 %psum.7 = f32[16,16]{1,0:T(8,128)} all-reduce(f32[16,16]{1,0:T(8,128)S(1)} %slice_add_fusion), channel_id=1, replica_groups=mesh['dp'=8,'feat'=4] {'feat'}, use_global_device_ids=true, to_apply=%region_3.4 | all-reduce | flops 256 | bytes 2048 | tf_op jit(solution)/shard_map/psum | solution.py:96
  (6 shorter events, 0.1 us)
Async XLA Ops:
  0.6 4.4 %copy-start.5 = (f32[32]{0:T(128)S(1)}, f32[32]{0:T(128)}, u32[]{:S(2)}) copy-start(f32[32]{0:T(128)} %param.19) | copy-start | bytes 388
  0.6 4.6 %copy-start.7 = (s32[128]{0:T(128)S(1)}, s32[128]{0:T(128)}, u32[]{:S(2)}) copy-start(s32[128]{0:T(128)} %param.13) | copy-start | bytes 1540
  0.7 4.7 %copy-start = (f32[16,512]{1,0:T(8,128)S(1)}, f32[16,512]{1,0:T(8,128)}, u32[]{:S(2)}) copy-start(f32[16,512]{1,0:T(8,128)} %param.15) | copy-start | bytes 98308
  0.7 4.6 %copy-start.1 = (f32[16,512]{1,0:T(8,128)S(1)}, f32[16,512]{1,0:T(8,128)}, u32[]{:S(2)}) copy-start(f32[16,512]{1,0:T(8,128)} %param.16) | copy-start | bytes 98308
  0.7 4.6 %copy-start.3 = (f32[16,512]{1,0:T(8,128)S(1)}, f32[16,512]{1,0:T(8,128)}, u32[]{:S(2)}) copy-start(f32[16,512]{1,0:T(8,128)} %param.14) | copy-start | bytes 98308
  0.7 79.8 %all-to-all-start = ((bf16[4,32,32,128]{3,2,1,0:T(8,128)(2,1)}), bf16[4,32,32,128]{3,2,1,0:T(8,128)(2,1)S(1)}, u32[]{:S(2)}, u32[]{:S(2)}) async-start(bf16[4,32,32,128]{3,2,1,0:T(8,128)(2,1)} %bitcast.31), calls=%async_computation | async-start | bytes 2097152 | tf_op jit(solution)/shard_map/all_to_all | solution.py:41
  5.3 101.7 %copy-start.2 = (f32[16,512]{1,0:T(8,128)}, f32[16,512]{1,0:T(8,128)S(1)}, u32[]{:S(2)}) copy-start(f32[16,512]{1,0:T(8,128)S(1)} %get-tuple-element.10) | copy-start | bytes 98308
  78.1 1.5 %copy-start.8 = (s32[128]{0:T(128)S(1)}, s32[128]{0:T(128)}, u32[]{:S(2)}) copy-start(s32[128]{0:T(128)} %param.12) | copy-start | bytes 1540
  85.2 3.7 %copy-start.6 = (f32[32]{0:T(128)S(1)}, f32[32]{0:T(128)}, u32[]{:S(2)}) copy-start(f32[32]{0:T(128)} %param.18) | copy-start | bytes 388
  86.2 20.9 %copy-start.4 = (f32[512]{0:T(512)S(1)}, f32[512]{0:T(512)}, u32[]{:S(2)}) copy-start(f32[512]{0:T(512)} %param.17) | copy-start | bytes 6148
  86.2 20.7 %all-to-all-start.1 = ((bf16[32,16,528]{2,1,0:T(8,128)(2,1)}), bf16[32,16,528]{2,1,0:T(8,128)(2,1)S(1)}, u32[]{:S(2)}, u32[]{:S(2)}) async-start(bf16[32,16,528]{2,1,0:T(8,128)(2,1)} %bitcast.14), calls=%async_computation.1 | async-start | bytes 1310720 | tf_op jit(solution)/shard_map/all_to_all | solution.py:86

commit v2 on v1

--- a/solution.py
+++ b/solution.py
@@ -47,8 +47,9 @@
     half_momentum = momentum - 0.5 * step_size * gradient
     moved_position = position + step_size * mass_full * half_momentum
     rounded = moved_position.astype(jnp.bfloat16)
-    table = lax.all_gather(rounded, ("feat", "dp"), axis=0, tiled=True)
-    table = table.reshape(parts, groups, block_width)
+    copies = jnp.broadcast_to(rounded[None], (owners, own_groups, block_width))
+    table = lax.all_to_all(copies, "dp", 0, 0, tiled=True).reshape(groups, block_width)
+    table = lax.all_gather(table, "feat", axis=0, tiled=False)
 
     start = part_index * share
     share_labels = lax.dynamic_slice_in_dim(labels, start, share, 0)
@@ -64,29 +65,28 @@
         "qtfc,qtfr->tcr", coeffs, share_obs, preferred_element_type=jnp.float32
     )
     residual, neg_loglik = likelihood(logits, share_labels, share_live)
+    all_residual = lax.all_gather(residual, "feat", axis=0, tiled=True)
     grad = jnp.einsum(
-        "qtfr,tcr->tqfc", share_obs, residual, preferred_element_type=jnp.float32
-    ).reshape(share, parts * block_width)
-    chooser = member.astype(jnp.float32)
+        "tfr,tcr->tfc", observations, all_residual, preferred_element_type=jnp.float32
+    ).reshape(tile_count, block_width)
+    group_order = jnp.arange(groups, dtype=jnp.int32)
+    chooser = (tile_group[:, None] == group_order[None, :]).astype(jnp.float32)
     group_grad = jnp.einsum(
         "tg,tw->gw", chooser, grad, precision=lax.Precision.HIGHEST,
         preferred_element_type=jnp.float32,
     ).astype(jnp.bfloat16)
     group_loglik = jnp.einsum(
-        "tg,tc->gc", chooser, neg_loglik, precision=lax.Precision.HIGHEST,
+        "tg,tc->gc", member.astype(jnp.float32), neg_loglik, precision=lax.Precision.HIGHEST,
         preferred_element_type=jnp.float32,
     )
     high = group_loglik.astype(jnp.bfloat16)
     low = (group_loglik - high.astype(jnp.float32)).astype(jnp.bfloat16)
-    pad = jnp.zeros((groups, parts - 2, chains), jnp.bfloat16)
-    tails = jnp.concatenate([high[:, None], low[:, None], pad], axis=1)
-    send = jnp.concatenate([group_grad.reshape(groups, parts, block_width), tails], axis=2)
-    send = send.reshape(owners, own_groups, parts, block_width + chains).transpose(0, 2, 1, 3)
-    send = send.reshape(owners * parts, own_groups, block_width + chains)
-    got = lax.all_to_all(send, ("dp", "feat"), 0, 0, tiled=True)
+    send = jnp.concatenate([group_grad, high, low], axis=1)
+    send = send.reshape(owners, own_groups, block_width + 2 * chains)
+    got = lax.all_to_all(send, "dp", 0, 0, tiled=True)
     summed = jnp.sum(got.astype(jnp.float32), axis=0)
     likelihood_grad = summed[:, :block_width]
-    own_loglik = summed[:, block_width:]
+    own_loglik = summed[:, block_width:block_width + chains] + summed[:, block_width + chains:]
 
     offset = moved_position - prior_mean
     new_gradient = likelihood_grad + prior_full * offset

time: 116 us -> 70.8 us (0.61)
  blocking collectives: 80.3 us -> 44.1 us
  waiting for transfers between devices: 17.8 us -> 8.03 us
  local copies, waits for them, and re-layouts: 3.54 us -> 5.11 us
  matrix products: 3.27 us -> 2.1 us
    all_gather x1 -> x2, blocking collectives: 72.7 us -> 23.2 us  [the longest x1 15.9 us: body(): table = lax.all_gather(table, 'feat', axis=0, tiled=False)]
    all_to_all x0 -> x1, blocking collectives: none -> 14.5 us  [body(): lax.all_to_all(copies, 'dp', 0, 0, tiled=True).reshape(groups, block_width)]
    all_to_all x1, waiting for transfers between devices: 17.8 us -> 8.03 us  [body(): got = lax.all_to_all(send, 'dp', 0, 0, tiled=True)]
    unnamed x18 -> x16, local copies, waits for them, and re-layouts: 0.04 us -> 1.89 us
  transfers between devices with their start and end apart: 2 -> 2, of which waited for: 1 -> 1; matrix products, arithmetic and copies ran while one was open for 2% -> 4% of each run, Pallas kernels for 0% -> 0%
where the time goes in v2:
time: 70.8 us; the launch traced here: 70.2 us
  blocking collectives  44.1 us (62%)
  waiting for transfers between devices  8.03 us (11%)
  starting transfers between devices  7.03 us (10%)
  local copies, waits for them, and re-layouts  5.11 us (7%)
  other arithmetic  3.11 us (4%)
  matrix products  2.1 us (3%)
  between operations  0.8 us (1%)
    all_gather x1, blocking collectives, body(): table = lax.all_gather(table, 'feat', axis=0, tiled=False)  15.9 us
    all_to_all x1, blocking collectives, body(): lax.all_to_all(copies, 'dp', 0, 0, tiled=True).reshape(groups, block_width)  14.5 us
    all_to_all x1, waiting for transfers between devices, body(): got = lax.all_to_all(send, 'dp', 0, 0, tiled=True)  8.03 us
    all_gather x1, blocking collectives, body(): all_residual = lax.all_gather(residual, 'feat', axis=0, tiled=True)  7.28 us
    psum x1, blocking collectives, body(): energy = lax.psum(quadratic + own_loglik, 'feat')  6.46 us
    all_to_all x1, starting transfers between devices, body(): lax.all_to_all(observations.reshape(parts, share, quarter, row_count), 'f...  3.52 us
    all_to_all x1, starting transfers between devices, body(): got = lax.all_to_all(send, 'dp', 0, 0, tiled=True)  3.51 us
    unnamed x16, local copies, waits for them, and re-layouts  1.89 us
  transfers between devices with their start and end apart: 2, of which 1 were waited for; matrix products, arithmetic and copies ran while one was open for 4% of the time, Pallas kernels for 0%

profile of v2, /device:TPU:0, one launch (start us, length us, event | category | flops | bytes accessed | tf_op | source)
XLA Modules:
  0.0 70.2 jit_solution(16148259240525972634)
XLA Ops:
  0.6 0.0 copy-start.1
  0.6 0.7 %broadcast_in_dim.22 = f32[32,16]{1,0:T(8,128)S(1)} broadcast(f32[32]{0:T(128)} %param.19), dimensions={0} | broadcast | bytes 2176 | tf_op jit(solution)/shard_map/broadcast_in_dim | solution.py:46
  1.4 0.1 reshape.55
  1.5 0.0 copy-done.1
  1.5 0.8 %fusion.16 = (bf16[16,512]{1,0:T(8,128)(2,1)S(1)}, f32[16,512]{1,0:T(8,128)S(1)}) fusion(f32[16,512]{1,0:T(8,128)} %param.14, f32[16,512]{1,0:T(8,128)S(1)} %copy-done.1, f32[16,512]{1,0:T(8,128)} %param.16, f32[512]{0:T(512)S(1)} %broadcast_multiply_fusion), kind=kLoop, calls=%fused_computation.35 | loop fusion | flops 40960 | bytes 149504 | tf_op jit(solution)/shard_map/convert_element_type | solution.py:49
  2.3 0.0 copy-start.3
  2.3 14.5 %all_to_all.15 = bf16[8,16,512]{2,1,0:T(8,128)(2,1)S(1)} all-to-all(bf16[8,16,512]{2,1,0:T(8,128)(2,1)S(1)} %broadcast_in_dim.40), channel_id=1, replica_groups=mesh['dp'=8,'feat'=4] {'dp'}, dimensions={0} | all-to-all | bytes 262144 | tf_op jit(solution)/shard_map/all_to_all | solution.py:51
  16.7 3.5 %all-to-all-start.1 = ((bf16[4,32,32,128]{3,2,1,0:T(8,128)(2,1)}), bf16[4,32,32,128]{3,2,1,0:T(8,128)(2,1)S(1)}, u32[]{:S(2)}, u32[]{:S(2)}) async-start(bf16[4,32,32,128]{3,2,1,0:T(8,128)(2,1)} %bitcast.21), calls=%async_computation.1 | async-start | bytes 2097152 | tf_op jit(solution)/shard_map/all_to_all | solution.py:41
  20.3 0.0 copy-start.5
  20.3 0.6 copy-done.5
  20.9 0.0 copy-start.7
  20.9 0.1 dynamic_slice.10
  21.0 0.6 copy-done.7
  21.6 0.1 dynamic_slice.9
  21.7 0.7 %dynamic-slice_convert_fusion = f32[32,128]{1,0:T(8,128)S(1)} fusion(s32[128,128]{1,0:T(8,128)} %param.11, s32[]{:T(128)S(6)} %select_n.16), kind=kLoop, calls=%fused_computation.24 | loop fusion | flops 4096 | bytes 32772 | tf_op jit(solution)/shard_map/convert_element_type | solution.py:12
  22.4 0.1 iota_compare_fusion.3
  22.5 15.9 %all_gather.6 = bf16[4,128,512]{2,1,0:T(8,128)(2,1)S(1)} all-gather(bf16[1,128,512]{2,1,0:T(8,128)(2,1)S(1)} %bitcast.24), channel_id=1, replica_groups=mesh['dp'=8,'feat'=4] {'feat'}, dimensions={0}, use_global_device_ids=true | all-gather | bytes 655360 | tf_op jit(solution)/shard_map/all_gather | solution.py:52
  38.3 0.2 fusion
  38.6 0.3 copy.29
  38.9 1.0 %copy.30 = bf16[4,32,32,16]{2,3,0,1:T(8,128)(2,1)S(1)} copy(bf16[4,32,32,16]{1,3,2,0:T(8,128)(2,1)S(1)} %bitcast.22) | data formatting | bytes 262144 | tf_op jit(solution)/shard_map/reshape | solution.py:63
  39.8 0.0 all-to-all-done.1
  39.9 0.0 copy-start
  39.9 0.6 select_convert_fusion
  40.5 0.2 subtract_convert_fusion
  40.7 0.1 copy.33
  40.8 0.1 copy.34
  40.9 7.3 %all_gather.7 = bf16[128,16,128]{2,1,0:T(8,128)(2,1)S(1)} all-gather(bf16[32,16,128]{2,1,0:T(8,128)(2,1)S(1)} %get-tuple-element.11), channel_id=1, replica_groups=mesh['dp'=8,'feat'=4] {'feat'}, dimensions={0}, use_global_device_ids=true | all-gather | bytes 655360 | tf_op jit(solution)/shard_map/all_gather | solution.py:68
  48.2 0.0 copy-done
  48.2 0.7 convolution_bitcast_fusion
  48.9 0.5 copy.32
  49.4 0.4 convolution_convert_fusion.1
  49.8 0.7 %pad_maximum_fusion = bf16[128,544]{1,0:T(8,128)(2,1)} fusion(bf16[128,16]{1,0:T(8,128)(2,1)S(1)} %copy.34, bf16[128,16]{1,0:T(8,128)(2,1)S(1)} %copy.33, bf16[128,512]{1,0:T(8,128)(2,1)S(1)} %convolution_convert_fusion.1), kind=kLoop, calls=%fused_computation.12 | loop fusion | flops 417792 | bytes 278528 | tf_op jit(solution)/shard_map/concatenate | solution.py:84
  50.5 0.0 copy-start.6
  50.5 3.5 %all-to-all-start.2 = ((bf16[8,16,544]{2,1,0:T(8,128)(2,1)}), bf16[8,16,544]{2,1,0:T(8,128)(2,1)S(1)}, u32[]{:S(2)}, u32[]{:S(2)}) async-start(bf16[8,16,544]{2,1,0:T(8,128)(2,1)} %bitcast.9), calls=%async_computation.2 | async-start | bytes 327680 | tf_op jit(solution)/shard_map/all_to_all | solution.py:86
  54.0 0.0 copy-done.6
  54.0 0.1 broadcast_in_dim.42
  54.1 0.1 mul.74
  54.2 0.0 copy-start.2
  54.2 8.0 %all-to-all-done.2 = bf16[8,16,544]{2,1,0:T(8,128)(2,1)S(1)} async-done(((bf16[8,16,544]{2,1,0:T(8,128)(2,1)}), bf16[8,16,544]{2,1,0:T(8,128)(2,1)S(1)}, u32[]{:S(2)}, u32[]{:S(2)}) %all-to-all-start.2) | async-done | bytes 139296 | tf_op jit(solution)/shard_map/all_to_all | solution.py:86
  62.2 0.0 copy-start.4
  62.3 0.0 copy-done.3
  62.3 0.0 copy-done.2
  62.3 0.6 copy-done.4
  62.9 0.6 fusion.7
  63.5 0.1 reshape.60
  63.7 0.1 fusion.13
  63.8 6.5 %psum.7 = f32[16,16]{1,0:T(8,128)} all-reduce(f32[16,16]{1,0:T(8,128)S(1)} %fusion.13), channel_id=1, replica_groups=mesh['dp'=8,'feat'=4] {'feat'}, use_global_device_ids=true, to_apply=%region_3.4 | all-reduce | flops 256 | bytes 2048 | tf_op jit(solution)/shard_map/psum | solution.py:96
  (4 shorter events, 0.1 us)
Async XLA Ops:
  0.6 0.8 %copy-start.1 = (f32[16,512]{1,0:T(8,128)S(1)}, f32[16,512]{1,0:T(8,128)}, u32[]{:S(2)}) copy-start(f32[16,512]{1,0:T(8,128)} %param.15) | copy-start | bytes 98308
  2.3 60.0 %copy-start.3 = (f32[16,512]{1,0:T(8,128)}, f32[16,512]{1,0:T(8,128)S(1)}, u32[]{:S(2)}) copy-start(f32[16,512]{1,0:T(8,128)S(1)} %get-tuple-element.10) | copy-start | bytes 98308
  16.7 23.1 %all-to-all-start.1 = ((bf16[4,32,32,128]{3,2,1,0:T(8,128)(2,1)}), bf16[4,32,32,128]{3,2,1,0:T(8,128)(2,1)S(1)}, u32[]{:S(2)}, u32[]{:S(2)}) async-start(bf16[4,32,32,128]{3,2,1,0:T(8,128)(2,1)} %bitcast.21), calls=%async_computation.1 | async-start | bytes 2097152 | tf_op jit(solution)/shard_map/all_to_all | solution.py:41
  20.3 0.7 copy-start.5
  20.9 0.7 copy-start.7
  39.9 8.4 %copy-start = (bf16[128,32,128]{2,1,0:T(8,128)(2,1)S(1)}, bf16[128,32,128]{2,1,0:T(8,128)(2,1)}, u32[]{:S(2)}) copy-start(bf16[128,32,128]{2,1,0:T(8,128)(2,1)} %param.10) | copy-start | bytes 3145732
  50.5 3.5 %copy-start.6 = (f32[32]{0:T(128)S(1)}, f32[32]{0:T(128)}, u32[]{:S(2)}) copy-start(f32[32]{0:T(128)} %param.18) | copy-start | bytes 388
  50.5 11.7 %all-to-all-start.2 = ((bf16[8,16,544]{2,1,0:T(8,128)(2,1)}), bf16[8,16,544]{2,1,0:T(8,128)(2,1)S(1)}, u32[]{:S(2)}, u32[]{:S(2)}) async-start(bf16[8,16,544]{2,1,0:T(8,128)(2,1)} %bitcast.9), calls=%async_computation.2 | async-start | bytes 327680 | tf_op jit(solution)/shard_map/all_to_all | solution.py:86
  54.2 8.1 %copy-start.2 = (f32[16,512]{1,0:T(8,128)S(1)}, f32[16,512]{1,0:T(8,128)}, u32[]{:S(2)}) copy-start(f32[16,512]{1,0:T(8,128)} %param.16) | copy-start | bytes 98308
  62.2 0.7 copy-start.4

commit v3 on v2

--- a/solution.py
+++ b/solution.py
@@ -15,6 +15,18 @@
         jnp.where(live_rows, jax.nn.softplus(logits) - targets * logits, 0.0), axis=2
     )
     return (residual, neg_loglik)
+
+
+def sum_over_feat(value):
+    parts = lax.axis_size("feat")
+    if parts & (parts - 1):
+        return lax.psum(value, "feat")
+    terms = [value] + [
+        lax.ppermute(value, "feat", [(i, i ^ k) for i in range(parts)]) for k in range(1, parts)
+    ]
+    while len(terms) > 1:
+        terms = [terms[i] + terms[i + 1] for i in range(0, len(terms), 2)]
+    return terms[0]
 
 
 def body(
@@ -38,10 +50,6 @@
     groups = owners * own_groups
     share = tile_count // parts
 
-    share_obs = lax.all_to_all(
-        observations.reshape(parts, share, quarter, row_count), "feat", 0, 0, tiled=True
-    )
-
     prior_full = jnp.repeat(prior_prec, chains)
     mass_full = jnp.repeat(inv_mass, chains)
     half_momentum = momentum - 0.5 * step_size * gradient
@@ -49,7 +57,6 @@
     rounded = moved_position.astype(jnp.bfloat16)
     copies = jnp.broadcast_to(rounded[None], (owners, own_groups, block_width))
     table = lax.all_to_all(copies, "dp", 0, 0, tiled=True).reshape(groups, block_width)
-    table = lax.all_gather(table, "feat", axis=0, tiled=False)
 
     start = part_index * share
     share_labels = lax.dynamic_slice_in_dim(labels, start, share, 0)
@@ -57,20 +64,26 @@
     share_group = lax.dynamic_slice_in_dim(tile_group, start, share, 0)
     member = share_group[:, None] == jnp.arange(groups, dtype=jnp.int32)[None, :]
 
+    group_order = jnp.arange(groups, dtype=jnp.int32)
+    belongs = tile_group[:, None] == group_order[None, :]
     coeffs = jnp.einsum(
-        "tg,qgw->qtw", member.astype(jnp.bfloat16), table, preferred_element_type=jnp.float32
+        "tg,gw->tw", belongs.astype(jnp.bfloat16), table, preferred_element_type=jnp.float32
     ).astype(jnp.bfloat16)
-    coeffs = coeffs.reshape(parts, share, quarter, chains)
-    logits = jnp.einsum(
-        "qtfc,qtfr->tcr", coeffs, share_obs, preferred_element_type=jnp.float32
-    )
+    coeffs = coeffs.reshape(tile_count, quarter, chains)
+    partial = jnp.einsum(
+        "tfc,tfr->tcr", coeffs, observations, preferred_element_type=jnp.float32
+    ).astype(jnp.bfloat16).reshape(parts, share, chains, row_count)
+    logits = lax.dynamic_index_in_dim(partial, part_index, 0, False).astype(jnp.float32)
+    for hop in range(1, parts):
+        piece = lax.dynamic_index_in_dim(partial, (part_index + hop) % parts, 0, False)
+        piece = lax.ppermute(piece, "feat", [(i, (i + hop) % parts) for i in range(parts)])
+        logits = logits + piece.astype(jnp.float32)
     residual, neg_loglik = likelihood(logits, share_labels, share_live)
     all_residual = lax.all_gather(residual, "feat", axis=0, tiled=True)
     grad = jnp.einsum(
         "tfr,tcr->tfc", observations, all_residual, preferred_element_type=jnp.float32
     ).reshape(tile_count, block_width)
-    group_order = jnp.arange(groups, dtype=jnp.int32)
-    chooser = (tile_group[:, None] == group_order[None, :]).astype(jnp.float32)
+    chooser = belongs.astype(jnp.float32)
     group_grad = jnp.einsum(
         "tg,tw->gw", chooser, grad, precision=lax.Precision.HIGHEST,
         preferred_element_type=jnp.float32,
@@ -93,7 +106,7 @@
     new_momentum = half_momentum - 0.5 * step_size * new_gradient
     quadratic = 0.5 * (prior_full * offset * offset + mass_full * new_momentum * new_momentum)
     quadratic = jnp.sum(quadratic.reshape(own_groups, quarter, chains), axis=1)
-    energy = lax.psum(quadratic + own_loglik, "feat")
+    energy = sum_over_feat(quadratic + own_loglik)
     return (moved_position, new_momentum, new_gradient, energy)
 
 

time: 70.8 us -> 55.6 us (0.79)
  blocking collectives: 44.1 us -> 7.73 us
  waiting for transfers between devices: 8.03 us -> 20.3 us
  starting transfers between devices: 7.03 us -> 15.7 us
  other arithmetic: 3.11 us -> 4.11 us
    all_gather x1 -> x0, blocking collectives: 15.9 us -> none  [body(): table = lax.all_gather(table, 'feat', axis=0, tiled=False)]
    all_to_all x1 -> x0, blocking collectives: 14.5 us -> none  [body(): lax.all_to_all(copies, 'dp', 0, 0, tiled=True).reshape(groups, block_width)]
    all_to_all x1, waiting for transfers between devices: 0.01 us -> 6.61 us  [body(): lax.all_to_all(copies, 'dp', 0, 0, tiled=True).reshape(groups, block_width)]
    psum x1 -> x0, blocking collectives: 6.46 us -> none  [body(): energy = lax.psum(quadratic + own_loglik, 'feat')]
    ppermute x0 -> x6, waiting for transfers between devices: none -> 5.66 us  [the longest x3 3.79 us: body(): lax.ppermute(piece, 'feat', [(i, (i + hop) % parts) for i in range(parts)])]
    ppermute x0 -> x6, starting transfers between devices: none -> 4.86 us  [the longest x3 3 us: body(): lax.ppermute(piece, 'feat', [(i, (i + hop) % parts) for i in range(parts)])]
    all_to_all x1, starting transfers between devices: 3.52 us -> 7.31 us  [body(): lax.all_to_all(copies, 'dp', 0, 0, tiled=True).reshape(groups, block_width)]
  transfers between devices with their start and end apart: 2 -> 8, of which waited for: 1 -> 6; matrix products, arithmetic and copies ran while one was open for 4% -> 2% of each run, Pallas kernels for 0% -> 0%
where the time goes in v3:
time: 55.6 us; the launch traced here: 55.2 us
  waiting for transfers between devices  20.3 us (37%)
  starting transfers between devices  15.7 us (28%)
  blocking collectives  7.73 us (14%)
  local copies, waits for them, and re-layouts  4.65 us (8%)
  other arithmetic  4.11 us (7%)
  matrix products  1.88 us (3%)
  between operations  0.81 us (1%)
    all_to_all x1, waiting for transfers between devices, body(): got = lax.all_to_all(send, 'dp', 0, 0, tiled=True)  8.03 us
    all_gather x1, blocking collectives, body(): all_residual = lax.all_gather(residual, 'feat', axis=0, tiled=True)  7.73 us
    all_to_all x1, starting transfers between devices, body(): lax.all_to_all(copies, 'dp', 0, 0, tiled=True).reshape(groups, block_width)  7.31 us
    all_to_all x1, waiting for transfers between devices, body(): lax.all_to_all(copies, 'dp', 0, 0, tiled=True).reshape(groups, block_width)  6.61 us
    ppermute x3, waiting for transfers between devices, body(): lax.ppermute(piece, 'feat', [(i, (i + hop) % parts) for i in range(parts)])  3.79 us
    all_to_all x1, starting transfers between devices, body(): got = lax.all_to_all(send, 'dp', 0, 0, tiled=True)  3.51 us
    ppermute x3, starting transfers between devices, body(): lax.ppermute(piece, 'feat', [(i, (i + hop) % parts) for i in range(parts)])  3 us
    ppermute x3, waiting for transfers between devices, sum_over_feat(): lax.ppermute(value, 'feat', [(i, i ^ k) for i in range(parts)])  1.87 us
  transfers between devices with their start and end apart: 8, of which 6 were waited for; matrix products, arithmetic and copies ran while one was open for 2% of the time, Pallas kernels for 0%

profile of v3, /device:TPU:0, one launch (start us, length us, event | category | flops | bytes accessed | tf_op | source)
XLA Modules:
  0.0 55.2 jit_solution(16098222222219288922)
XLA Ops:
  0.6 0.0 copy-start
  0.6 0.0 copy-start.1
  0.7 0.8 %broadcast_in_dim.18 = f32[32,16]{1,0:T(8,128)S(1)} broadcast(f32[32]{0:T(128)} %param.19), dimensions={0} | broadcast | bytes 2176 | tf_op jit(solution)/shard_map/broadcast_in_dim | solution.py:54
  1.5 0.1 reshape.60
  1.6 0.8 %fusion.14 = (bf16[16,512]{1,0:T(8,128)(2,1)S(1)}, f32[16,512]{1,0:T(8,128)S(1)}) fusion(f32[16,512]{1,0:T(8,128)} %param.14, f32[16,512]{1,0:T(8,128)S(1)} %copy-done.1, f32[16,512]{1,0:T(8,128)} %param.16, f32[512]{0:T(512)S(1)} %broadcast_multiply_fusion), kind=kLoop, calls=%fused_computation.39 | loop fusion | flops 40960 | bytes 149504 | tf_op jit(solution)/shard_map/convert_element_type | solution.py:57
  2.4 0.0 copy-start.3
  2.4 0.7 %broadcast_in_dim.40 = bf16[8,16,512]{2,1,0:T(8,128)(2,1)} broadcast(bf16[16,512]{1,0:T(8,128)(2,1)S(1)} %get-tuple-element.9), dimensions={1,2} | broadcast | bytes 147456 | tf_op jit(solution)/shard_map/broadcast_in_dim | solution.py:58
  3.0 7.3 %all-to-all-start = ((bf16[8,16,512]{2,1,0:T(8,128)(2,1)}), bf16[8,16,512]{2,1,0:T(8,128)(2,1)S(1)}, u32[]{:S(2)}, u32[]{:S(2)}) async-start(bf16[8,16,512]{2,1,0:T(8,128)(2,1)} %broadcast_in_dim.40), calls=%async_computation | async-start | bytes 262144 | tf_op jit(solution)/shard_map/all_to_all | solution.py:59
  10.3 0.7 %copy-done.7 = s32[128]{0:T(128)S(1)} copy-done((s32[128]{0:T(128)S(1)}, s32[128]{0:T(128)}, u32[]{:S(2)}) %copy-start.7) | copy-done | bytes 536
  11.0 0.1 dynamic_slice.22
  11.1 6.6 %all-to-all-done = bf16[8,16,512]{2,1,0:T(8,128)(2,1)S(1)} async-done(((bf16[8,16,512]{2,1,0:T(8,128)(2,1)}), bf16[8,16,512]{2,1,0:T(8,128)(2,1)S(1)}, u32[]{:S(2)}, u32[]{:S(2)}) %all-to-all-start) | async-done | bytes 131104 | tf_op jit(solution)/shard_map/all_to_all | solution.py:59
  17.7 0.2 convolution_convert_fusion.2
  17.9 0.1 copy.27
  18.0 0.5 copy.28
  18.5 0.4 convolution_convert_fusion
  19.0 0.1 collective-permute-start
  19.1 1.6 %collective-permute-start.1 = (bf16[32,16,128]{2,1,0:T(8,128)(2,1)S(1)}, bf16[32,16,128]{2,1,0:T(8,128)(2,1)S(1)}, u32[]{:S(2)}, u32[]{:S(2)}) collective-permute-start(bf16[32,16,128]{2,1,0:T(8,128)(2,1)S(1)} %get-tuple-element.15), channel_id=1, source_target_pairs={{0,2},{1,3},{2,0},{3,1},{4,6},{5,7},{6,4},{7,5},{8,10},{9,11},{10,... | collective-permute-start | bytes 393224 | tf_op jit(solution)/shard_map/ppermute | solution.py:79
  20.6 1.4 %collective-permute-start.2 = (bf16[32,16,128]{2,1,0:T(8,128)(2,1)S(1)}, bf16[32,16,128]{2,1,0:T(8,128)(2,1)S(1)}, u32[]{:S(2)}, u32[]{:S(2)}) collective-permute-start(bf16[32,16,128]{2,1,0:T(8,128)(2,1)S(1)} %get-tuple-element.14), channel_id=1, source_target_pairs={{0,3},{1,0},{2,1},{3,2},{4,7},{5,4},{6,5},{7,6},{8,11},{9,8},{10,9... | collective-permute-start | bytes 393224 | tf_op jit(solution)/shard_map/ppermute | solution.py:79
  22.0 0.1 iota_compare_fusion.3
  22.1 0.1 dynamic_slice.28
  22.2 0.7 %dynamic-slice_convert_fusion = f32[32,128]{1,0:T(8,128)S(1)} fusion(s32[128,128]{1,0:T(8,128)} %param.11, s32[]{:T(128)S(6)} %select_n.44), kind=kLoop, calls=%fused_computation.30 | loop fusion | flops 4096 | bytes 32772 | tf_op jit(solution)/shard_map/convert_element_type | solution.py:12
  22.9 1.3 %collective-permute-done = bf16[32,16,128]{2,1,0:T(8,128)(2,1)S(1)} collective-permute-done((bf16[32,16,128]{2,1,0:T(8,128)(2,1)S(1)}, bf16[32,16,128]{2,1,0:T(8,128)(2,1)S(1)}, u32[]{:S(2)}, u32[]{:S(2)}) %collective-permute-start) | collective-permute-done | bytes 131104 | tf_op jit(solution)/shard_map/ppermute | solution.py:79
  24.2 1.3 %collective-permute-done.1 = bf16[32,16,128]{2,1,0:T(8,128)(2,1)S(1)} collective-permute-done((bf16[32,16,128]{2,1,0:T(8,128)(2,1)S(1)}, bf16[32,16,128]{2,1,0:T(8,128)(2,1)S(1)}, u32[]{:S(2)}, u32[]{:S(2)}) %collective-permute-start.1) | collective-permute-done | bytes 131104 | tf_op jit(solution)/shard_map/ppermute | solution.py:79
  25.5 1.2 %collective-permute-done.2 = bf16[32,16,128]{2,1,0:T(8,128)(2,1)S(1)} collective-permute-done((bf16[32,16,128]{2,1,0:T(8,128)(2,1)S(1)}, bf16[32,16,128]{2,1,0:T(8,128)(2,1)S(1)}, u32[]{:S(2)}, u32[]{:S(2)}) %collective-permute-start.2) | collective-permute-done | bytes 131104 | tf_op jit(solution)/shard_map/ppermute | solution.py:79
  26.7 0.4 select_convert_fusion
  27.0 7.7 %all_gather.3 = bf16[128,16,128]{2,1,0:T(8,128)(2,1)S(1)} all-gather(bf16[32,16,128]{2,1,0:T(8,128)(2,1)S(1)} %get-tuple-element.11), channel_id=1, replica_groups=mesh['dp'=8,'feat'=4] {'feat'}, dimensions={0}, use_global_device_ids=true | all-gather | bytes 655360 | tf_op jit(solution)/shard_map/all_gather | solution.py:82
  34.8 0.7 %convolution_bitcast_fusion = f32[128,32,16]{1,2,0:T(8,128)S(1)} fusion(bf16[128,16,128]{2,1,0:T(8,128)(2,1)S(1)} %all_gather.3, bf16[128,32,128]{2,1,0:T(8,128)(2,1)S(1)} %copy-done), kind=kOutput, calls=%fused_computation | convolution fusion | flops 16777216 | bytes 1835008 | tf_op jit(solution)/shard_map/tfr,tcr->tfc/dot_general | solution.py:83
  35.4 0.5 copy.29
  35.9 0.4 convolution_convert_fusion.1
  36.3 0.2 subtract_convert_fusion
  36.5 0.1 copy.30
  36.6 0.1 copy.31
  36.8 0.8 %pad_maximum_fusion = bf16[128,544]{1,0:T(8,128)(2,1)} fusion(bf16[128,16]{1,0:T(8,128)(2,1)S(1)} %copy.31, bf16[128,16]{1,0:T(8,128)(2,1)S(1)} %copy.30, bf16[128,512]{1,0:T(8,128)(2,1)S(1)} %convolution_convert_fusion.1), kind=kLoop, calls=%fused_computation.13 | loop fusion | flops 417792 | bytes 278528 | tf_op jit(solution)/shard_map/concatenate | solution.py:97
  37.5 3.5 %all-to-all-start.1 = ((bf16[8,16,544]{2,1,0:T(8,128)(2,1)}), bf16[8,16,544]{2,1,0:T(8,128)(2,1)S(1)}, u32[]{:S(2)}, u32[]{:S(2)}) async-start(bf16[8,16,544]{2,1,0:T(8,128)(2,1)} %bitcast.9), calls=%async_computation.1 | async-start | bytes 327680 | tf_op jit(solution)/shard_map/all_to_all | solution.py:99
  41.1 0.1 broadcast_in_dim.42
  41.1 0.1 mul.74
  41.2 8.0 %all-to-all-done.1 = bf16[8,16,544]{2,1,0:T(8,128)(2,1)S(1)} async-done(((bf16[8,16,544]{2,1,0:T(8,128)(2,1)}), bf16[8,16,544]{2,1,0:T(8,128)(2,1)S(1)}, u32[]{:S(2)}, u32[]{:S(2)}) %all-to-all-start.1) | async-done | bytes 139296 | tf_op jit(solution)/shard_map/all_to_all | solution.py:99
  49.3 0.6 %copy-done.4 = f32[512]{0:T(512)S(1)} copy-done((f32[512]{0:T(512)S(1)}, f32[512]{0:T(512)}, u32[]{:S(2)}) %copy-start.4) | copy-done | bytes 2072
  49.9 0.6 %fusion.7 = (f32[16,512]{1,0:T(8,128)S(1)}, f32[16,512]{1,0:T(8,128)}, f32[16,512]{1,0:T(8,128)}) fusion(f32[16,512]{1,0:T(8,128)S(1)} %get-tuple-element.10, f32[512]{0:T(512)S(1)} %reshape.60, f32[512]{0:T(512)S(1)} %copy-done.4, f32[512]{0:T(512)S(1)} %mul.74, f32[16,512]{1,0:T(8,128)S(1)} %copy-done.1, f32[16,512]{1,0:T(8,128)S(1)} %copy-done.2, ...), kind=kLoop, calls=%fused_computation.23 | loop fusion | flops 98304 | bytes 235520 | tf_op jit(solution)/shard_map/mul | solution.py:107
  50.6 0.1 reshape.66
  50.7 0.1 fusion.12
  50.8 0.0 collective-permute-start.3
  50.8 0.5 collective-permute-start.4
  51.3 1.4 %collective-permute-start.5 = (f32[16,16]{1,0:T(8,128)S(1)}, f32[16,16]{1,0:T(8,128)S(1)}, u32[]{:S(2)}, u32[]{:S(2)}) collective-permute-start(f32[16,16]{1,0:T(8,128)S(1)} %fusion.12), channel_id=1, source_target_pairs={{0,3},{1,2},{2,1},{3,0},{4,7},{5,6},{6,5},{7,4},{8,11},{9,10},{10,... | collective-permute-start | bytes 3080 | tf_op jit(solution)/shard_map/ppermute | solution.py:25
  52.7 0.0 collective-permute-done.3
  52.7 1.9 %collective-permute-done.4 = f32[16,16]{1,0:T(8,128)S(1)} collective-permute-done((f32[16,16]{1,0:T(8,128)S(1)}, f32[16,16]{1,0:T(8,128)S(1)}, u32[]{:S(2)}, u32[]{:S(2)}) %collective-permute-start.4) | collective-permute-done | bytes 1056 | tf_op jit(solution)/shard_map/ppermute | solution.py:25
  54.6 0.0 collective-permute-done.5
  54.6 0.6 %add_add_fusion = f32[16,16]{1,0:T(8,128)} fusion(f32[16,16]{1,0:T(8,128)S(1)} %collective-permute-done.4, f32[16,16]{1,0:T(8,128)S(1)} %collective-permute-done.5, f32[16,16]{1,0:T(8,128)S(1)} %fusion.12, f32[16,16]{1,0:T(8,128)S(1)} %collective-permute-done.3), kind=kLoop, calls=%fused_computation.35 | loop fusion | flops 768 | bytes 5120 | tf_op jit(solution)/shard_map/add | solution.py:28
  (15 shorter events, 0.1 us)
Async XLA Ops:
  0.6 17.9 %copy-start = (bf16[128,32,128]{2,1,0:T(8,128)(2,1)S(1)}, bf16[128,32,128]{2,1,0:T(8,128)(2,1)}, u32[]{:S(2)}) copy-start(bf16[128,32,128]{2,1,0:T(8,128)(2,1)} %param.10) | copy-start | bytes 3145732
  0.6 0.9 %copy-start.1 = (f32[16,512]{1,0:T(8,128)S(1)}, f32[16,512]{1,0:T(8,128)}, u32[]{:S(2)}) copy-start(f32[16,512]{1,0:T(8,128)} %param.15) | copy-start | bytes 98308
  2.4 46.9 %copy-start.3 = (f32[16,512]{1,0:T(8,128)}, f32[16,512]{1,0:T(8,128)S(1)}, u32[]{:S(2)}) copy-start(f32[16,512]{1,0:T(8,128)S(1)} %get-tuple-element.10) | copy-start | bytes 98308
  3.0 14.7 %all-to-all-start = ((bf16[8,16,512]{2,1,0:T(8,128)(2,1)}), bf16[8,16,512]{2,1,0:T(8,128)(2,1)S(1)}, u32[]{:S(2)}, u32[]{:S(2)}) async-start(bf16[8,16,512]{2,1,0:T(8,128)(2,1)} %broadcast_in_dim.40), calls=%async_computation | async-start | bytes 262144 | tf_op jit(solution)/shard_map/all_to_all | solution.py:59
  10.3 0.7 %copy-start.7 = (s32[128]{0:T(128)S(1)}, s32[128]{0:T(128)}, u32[]{:S(2)}) copy-start(s32[128]{0:T(128)} %param.12) | copy-start | bytes 1540
  11.1 6.6 %copy-start.5 = (s32[128]{0:T(128)S(1)}, s32[128]{0:T(128)}, u32[]{:S(2)}) copy-start(s32[128]{0:T(128)} %param.13) | copy-start | bytes 1540
  19.0 5.2 %collective-permute-start = (bf16[32,16,128]{2,1,0:T(8,128)(2,1)S(1)}, bf16[32,16,128]{2,1,0:T(8,128)(2,1)S(1)}, u32[]{:S(2)}, u32[]{:S(2)}) collective-permute-start(bf16[32,16,128]{2,1,0:T(8,128)(2,1)S(1)} %get-tuple-element.13), channel_id=1, source_target_pairs={{0,1},{1,2},{2,3},{3,0},{4,5},{5,6},{6,7},{7,4},{8,9},{9,10},{10,1... | collective-permute-start | bytes 393224 | tf_op jit(solution)/shard_map/ppermute | solution.py:79
  19.1 6.4 %collective-permute-start.1 = (bf16[32,16,128]{2,1,0:T(8,128)(2,1)S(1)}, bf16[32,16,128]{2,1,0:T(8,128)(2,1)S(1)}, u32[]{:S(2)}, u32[]{:S(2)}) collective-permute-start(bf16[32,16,128]{2,1,0:T(8,128)(2,1)S(1)} %get-tuple-element.15), channel_id=1, source_target_pairs={{0,2},{1,3},{2,0},{3,1},{4,6},{5,7},{6,4},{7,5},{8,10},{9,11},{10,... | collective-permute-start | bytes 393224 | tf_op jit(solution)/shard_map/ppermute | solution.py:79
  20.6 6.0 %collective-permute-start.2 = (bf16[32,16,128]{2,1,0:T(8,128)(2,1)S(1)}, bf16[32,16,128]{2,1,0:T(8,128)(2,1)S(1)}, u32[]{:S(2)}, u32[]{:S(2)}) collective-permute-start(bf16[32,16,128]{2,1,0:T(8,128)(2,1)S(1)} %get-tuple-element.14), channel_id=1, source_target_pairs={{0,3},{1,0},{2,1},{3,2},{4,7},{5,4},{6,5},{7,6},{8,11},{9,8},{10,9... | collective-permute-start | bytes 393224 | tf_op jit(solution)/shard_map/ppermute | solution.py:79
  37.5 3.5 %copy-start.6 = (f32[32]{0:T(128)S(1)}, f32[32]{0:T(128)}, u32[]{:S(2)}) copy-start(f32[32]{0:T(128)} %param.18) | copy-start | bytes 388
  37.5 11.7 %all-to-all-start.1 = ((bf16[8,16,544]{2,1,0:T(8,128)(2,1)}), bf16[8,16,544]{2,1,0:T(8,128)(2,1)S(1)}, u32[]{:S(2)}, u32[]{:S(2)}) async-start(bf16[8,16,544]{2,1,0:T(8,128)(2,1)} %bitcast.9), calls=%async_computation.1 | async-start | bytes 327680 | tf_op jit(solution)/shard_map/all_to_all | solution.py:99
  41.2 8.1 %copy-start.2 = (f32[16,512]{1,0:T(8,128)S(1)}, f32[16,512]{1,0:T(8,128)}, u32[]{:S(2)}) copy-start(f32[16,512]{1,0:T(8,128)} %param.16) | copy-start | bytes 98308
  49.3 0.7 %copy-start.4 = (f32[512]{0:T(512)S(1)}, f32[512]{0:T(512)}, u32[]{:S(2)}) copy-start(f32[512]{0:T(512)} %param.17) | copy-start | bytes 6148
  50.8 1.9 %collective-permute-start.3 = (f32[16,16]{1,0:T(8,128)S(1)}, f32[16,16]{1,0:T(8,128)S(1)}, u32[]{:S(2)}, u32[]{:S(2)}) collective-permute-start(f32[16,16]{1,0:T(8,128)S(1)} %fusion.12), channel_id=1, source_target_pairs={{0,1},{1,0},{2,3},{3,2},{4,5},{5,4},{6,7},{7,6},{8,9},{9,8},{10,11... | collective-permute-start | bytes 3080 | tf_op jit(solution)/shard_map/ppermute | solution.py:25
  50.8 3.7 %collective-permute-start.4 = (f32[16,16]{1,0:T(8,128)S(1)}, f32[16,16]{1,0:T(8,128)S(1)}, u32[]{:S(2)}, u32[]{:S(2)}) collective-permute-start(f32[16,16]{1,0:T(8,128)S(1)} %fusion.12), channel_id=1, source_target_pairs={{0,2},{1,3},{2,0},{3,1},{4,6},{5,7},{6,4},{7,5},{8,10},{9,11},{10,... | collective-permute-start | bytes 3080 | tf_op jit(solution)/shard_map/ppermute | solution.py:25
  51.3 3.2 %collective-permute-start.5 = (f32[16,16]{1,0:T(8,128)S(1)}, f32[16,16]{1,0:T(8,128)S(1)}, u32[]{:S(2)}, u32[]{:S(2)}) collective-permute-start(f32[16,16]{1,0:T(8,128)S(1)} %fusion.12), channel_id=1, source_target_pairs={{0,3},{1,2},{2,1},{3,0},{4,7},{5,6},{6,5},{7,4},{8,11},{9,10},{10,... | collective-permute-start | bytes 3080 | tf_op jit(solution)/shard_map/ppermute | solution.py:25

commit v4 on v3

--- a/solution.py
+++ b/solution.py
@@ -1,6 +1,7 @@
 import jax
 import jax.numpy as jnp
 from jax import lax
+from jax.experimental import pallas as pl
 from jax.sharding import PartitionSpec as P
 
 step_size = 0.1
@@ -29,6 +30,39 @@
     return terms[0]
 
 
+def opening(position, momentum, gradient, inv_mass, owners):
+    own_groups, width = position.shape
+    quarter = inv_mass.shape[0]
+    chains = width // quarter
+
+    def kernel(mass_ref, position_ref, momentum_ref, gradient_ref, half_ref, moved_ref, copies_ref):
+        feature = lax.broadcasted_iota(jnp.int32, (quarter, width), 0)
+        entry = lax.broadcasted_iota(jnp.int32, (quarter, width), 1)
+        first = feature * chains
+        spread = ((entry >= first) & (entry < first + chains)).astype(jnp.float32)
+        mass = jnp.dot(
+            mass_ref[...], spread, precision=lax.Precision.HIGHEST,
+            preferred_element_type=jnp.float32,
+        )
+        half = momentum_ref[...] - 0.5 * step_size * gradient_ref[...]
+        moved = position_ref[...] + step_size * mass * half
+        half_ref[...] = half
+        moved_ref[...] = moved
+        rounded = moved.astype(jnp.bfloat16)
+        for owner in range(copies_ref.shape[0]):
+            copies_ref[owner] = rounded
+
+    return pl.pallas_call(
+        kernel,
+        out_shape=(
+            jax.ShapeDtypeStruct((own_groups, width), jnp.float32),
+            jax.ShapeDtypeStruct((own_groups, width), jnp.float32),
+            jax.ShapeDtypeStruct((owners, own_groups, width), jnp.bfloat16),
+        ),
+        name="opening",
+    )(inv_mass[None], position, momentum, gradient)
+
+
 def body(
     observations,
     labels,
@@ -52,10 +86,9 @@
 
     prior_full = jnp.repeat(prior_prec, chains)
     mass_full = jnp.repeat(inv_mass, chains)
-    half_momentum = momentum - 0.5 * step_size * gradient
-    moved_position = position + step_size * mass_full * half_momentum
-    rounded = moved_position.astype(jnp.bfloat16)
-    copies = jnp.broadcast_to(rounded[None], (owners, own_groups, block_width))
+    half_momentum, moved_position, copies = opening(
+        position, momentum, gradient, inv_mass, owners
+    )
     table = lax.all_to_all(copies, "dp", 0, 0, tiled=True).reshape(groups, block_width)
 
     start = part_index * share

time: 55.6 us -> 55 us (0.989)
  Pallas kernels: 0 us -> 1.73 us
  local copies, waits for them, and re-layouts: 4.65 us -> 3.84 us
  other arithmetic: 4.11 us -> 3.31 us
  waiting for transfers between devices: 20.3 us -> 19.6 us
    pallas_call x0 -> x1, Pallas kernels: none -> 1.73 us  [opening(): pl.pallas_call(kernel, out_shape=(jax.ShapeDtypeStruct((own_groups, width...]
    convert_element_type x1 -> x0, other arithmetic: 0.79 us -> none  [body(): rounded = moved_position.astype(jnp.bfloat16)]
    broadcast_in_dim x1, local copies, waits for them, and re-layouts: 0.82 us -> 0.07 us  [body(): mass_full = jnp.repeat(inv_mass, chains)]
    all_to_all x1, waiting for transfers between devices: 8.03 us -> 7.3 us  [body(): got = lax.all_to_all(send, 'dp', 0, 0, tiled=True)]
    broadcast_in_dim x1 -> x0, local copies, waits for them, and re-layouts: 0.66 us -> none  [body(): copies = jnp.broadcast_to(rounded[None], (owners, own_groups, block_width))]
    unnamed x16, local copies, waits for them, and re-layouts: 1.31 us -> 1.91 us
where the time goes in v4:
time: 55 us; the launch traced here: 54.5 us
  waiting for transfers between devices  19.6 us (36%)
  starting transfers between devices  15.7 us (29%)
  blocking collectives  7.73 us (14%)
  local copies, waits for them, and re-layouts  3.84 us (7%)
  other arithmetic  3.31 us (6%)
  matrix products  1.88 us (3%)
  Pallas kernels  1.73 us (3%)
  between operations  0.8 us (1%)
    all_gather x1, blocking collectives, body(): all_residual = lax.all_gather(residual, 'feat', axis=0, tiled=True)  7.73 us
    all_to_all x1, starting transfers between devices, body(): lax.all_to_all(copies, 'dp', 0, 0, tiled=True).reshape(groups, block_width)  7.31 us
    all_to_all x1, waiting for transfers between devices, body(): got = lax.all_to_all(send, 'dp', 0, 0, tiled=True)  7.3 us
    all_to_all x1, waiting for transfers between devices, body(): lax.all_to_all(copies, 'dp', 0, 0, tiled=True).reshape(groups, block_width)  6.61 us
    ppermute x3, waiting for transfers between devices, body(): lax.ppermute(piece, 'feat', [(i, (i + hop) % parts) for i in range(parts)])  3.79 us
    all_to_all x1, starting transfers between devices, body(): got = lax.all_to_all(send, 'dp', 0, 0, tiled=True)  3.51 us
    ppermute x3, starting transfers between devices, body(): lax.ppermute(piece, 'feat', [(i, (i + hop) % parts) for i in range(parts)])  3 us
    unnamed x16, local copies, waits for them, and re-layouts  1.91 us
  transfers between devices with their start and end apart: 8, of which 6 were waited for; matrix products, arithmetic and copies ran while one was open for 2% of the time, Pallas kernels for 0%

profile of v4, /device:TPU:0, one launch (start us, length us, event | category | flops | bytes accessed | tf_op | source)
XLA Modules:
  0.0 54.5 jit_solution(5558130081160834163)
XLA Ops:
  0.6 0.0 copy-start
  0.6 1.7 %opening.1 = (f32[16,512]{1,0:T(8,128)}, f32[16,512]{1,0:T(8,128)}, bf16[8,16,512]{2,1,0:T(8,128)(2,1)}) custom-call(f32[1,32]{1,0:T(1,128)} %bitcast.33, f32[16,512]{1,0:T(8,128)} %position_ref.1, f32[16,512]{1,0:T(8,128)} %momentum_ref.1, f32[16,512]{1,0:T(8,128)} %gradient_ref.1), custom_call_target="tpu_custom_call" | custom-call | tf_op jit(solution)/shard_map/opening/pallas_call | solution.py:55
  2.4 7.3 %all-to-all-start = ((bf16[8,16,512]{2,1,0:T(8,128)(2,1)}), bf16[8,16,512]{2,1,0:T(8,128)(2,1)S(1)}, u32[]{:S(2)}, u32[]{:S(2)}) async-start(bf16[8,16,512]{2,1,0:T(8,128)(2,1)} %get-tuple-element.9), calls=%async_computation | async-start | bytes 262144 | tf_op jit(solution)/shard_map/all_to_all | solution.py:92
  9.7 0.7 %copy-done.7 = s32[128]{0:T(128)S(1)} copy-done((s32[128]{0:T(128)S(1)}, s32[128]{0:T(128)}, u32[]{:S(2)}) %copy-start.7) | copy-done | bytes 536
  10.3 0.1 dynamic_slice.22
  10.4 6.6 %all-to-all-done = bf16[8,16,512]{2,1,0:T(8,128)(2,1)S(1)} async-done(((bf16[8,16,512]{2,1,0:T(8,128)(2,1)}), bf16[8,16,512]{2,1,0:T(8,128)(2,1)S(1)}, u32[]{:S(2)}, u32[]{:S(2)}) %all-to-all-start) | async-done | bytes 131104 | tf_op jit(solution)/shard_map/all_to_all | solution.py:92
  17.0 0.2 convolution_convert_fusion.2
  17.3 0.1 copy.27
  17.4 0.5 copy.28
  17.9 0.0 copy-done
  17.9 0.4 convolution_convert_fusion
  18.3 0.1 collective-permute-start
  18.4 1.6 %collective-permute-start.1 = (bf16[32,16,128]{2,1,0:T(8,128)(2,1)S(1)}, bf16[32,16,128]{2,1,0:T(8,128)(2,1)S(1)}, u32[]{:S(2)}, u32[]{:S(2)}) collective-permute-start(bf16[32,16,128]{2,1,0:T(8,128)(2,1)S(1)} %get-tuple-element.19), channel_id=1, source_target_pairs={{0,2},{1,3},{2,0},{3,1},{4,6},{5,7},{6,4},{7,5},{8,10},{9,11},{10,... | collective-permute-start | bytes 393224 | tf_op jit(solution)/shard_map/ppermute | solution.py:112
  20.0 1.4 %collective-permute-start.2 = (bf16[32,16,128]{2,1,0:T(8,128)(2,1)S(1)}, bf16[32,16,128]{2,1,0:T(8,128)(2,1)S(1)}, u32[]{:S(2)}, u32[]{:S(2)}) collective-permute-start(bf16[32,16,128]{2,1,0:T(8,128)(2,1)S(1)} %get-tuple-element.18), channel_id=1, source_target_pairs={{0,3},{1,0},{2,1},{3,2},{4,7},{5,4},{6,5},{7,6},{8,11},{9,8},{10,9... | collective-permute-start | bytes 393224 | tf_op jit(solution)/shard_map/ppermute | solution.py:112
  21.3 0.1 iota_compare_fusion.3
  21.4 0.1 dynamic_slice.28
  21.5 0.7 %dynamic-slice_convert_fusion = f32[32,128]{1,0:T(8,128)S(1)} fusion(s32[128,128]{1,0:T(8,128)} %param.11, s32[]{:T(128)S(6)} %select_n.44), kind=kLoop, calls=%fused_computation.28 | loop fusion | flops 4096 | bytes 32772 | tf_op jit(solution)/shard_map/convert_element_type | solution.py:13
  22.2 1.3 %collective-permute-done = bf16[32,16,128]{2,1,0:T(8,128)(2,1)S(1)} collective-permute-done((bf16[32,16,128]{2,1,0:T(8,128)(2,1)S(1)}, bf16[32,16,128]{2,1,0:T(8,128)(2,1)S(1)}, u32[]{:S(2)}, u32[]{:S(2)}) %collective-permute-start) | collective-permute-done | bytes 131104 | tf_op jit(solution)/shard_map/ppermute | solution.py:112
  23.5 1.3 %collective-permute-done.1 = bf16[32,16,128]{2,1,0:T(8,128)(2,1)S(1)} collective-permute-done((bf16[32,16,128]{2,1,0:T(8,128)(2,1)S(1)}, bf16[32,16,128]{2,1,0:T(8,128)(2,1)S(1)}, u32[]{:S(2)}, u32[]{:S(2)}) %collective-permute-start.1) | collective-permute-done | bytes 131104 | tf_op jit(solution)/shard_map/ppermute | solution.py:112
  24.8 1.2 %collective-permute-done.2 = bf16[32,16,128]{2,1,0:T(8,128)(2,1)S(1)} collective-permute-done((bf16[32,16,128]{2,1,0:T(8,128)(2,1)S(1)}, bf16[32,16,128]{2,1,0:T(8,128)(2,1)S(1)}, u32[]{:S(2)}, u32[]{:S(2)}) %collective-permute-start.2) | collective-permute-done | bytes 131104 | tf_op jit(solution)/shard_map/ppermute | solution.py:112
  26.0 0.4 select_convert_fusion
  26.4 7.7 %all_gather.3 = bf16[128,16,128]{2,1,0:T(8,128)(2,1)S(1)} all-gather(bf16[32,16,128]{2,1,0:T(8,128)(2,1)S(1)} %get-tuple-element.15), channel_id=1, replica_groups=mesh['dp'=8,'feat'=4] {'feat'}, dimensions={0}, use_global_device_ids=true | all-gather | bytes 655360 | tf_op jit(solution)/shard_map/all_gather | solution.py:115
  34.1 0.7 %convolution_bitcast_fusion = f32[128,32,16]{1,2,0:T(8,128)S(1)} fusion(bf16[128,16,128]{2,1,0:T(8,128)(2,1)S(1)} %all_gather.3, bf16[128,32,128]{2,1,0:T(8,128)(2,1)S(1)} %copy-done), kind=kOutput, calls=%fused_computation | convolution fusion | flops 16777216 | bytes 1835008 | tf_op jit(solution)/shard_map/tfr,tcr->tfc/dot_general | solution.py:116
  34.8 0.5 copy.29
  35.3 0.4 convolution_convert_fusion.1
  35.7 0.2 subtract_convert_fusion
  35.9 0.1 copy.30
  36.0 0.1 copy.31
  36.1 0.8 %pad_maximum_fusion = bf16[128,544]{1,0:T(8,128)(2,1)} fusion(bf16[128,16]{1,0:T(8,128)(2,1)S(1)} %copy.31, bf16[128,16]{1,0:T(8,128)(2,1)S(1)} %copy.30, bf16[128,512]{1,0:T(8,128)(2,1)S(1)} %convolution_convert_fusion.1), kind=kLoop, calls=%fused_computation.13 | loop fusion | flops 417792 | bytes 278528 | tf_op jit(solution)/shard_map/concatenate | solution.py:130
  36.9 3.5 %all-to-all-start.1 = ((bf16[8,16,544]{2,1,0:T(8,128)(2,1)}), bf16[8,16,544]{2,1,0:T(8,128)(2,1)S(1)}, u32[]{:S(2)}, u32[]{:S(2)}) async-start(bf16[8,16,544]{2,1,0:T(8,128)(2,1)} %bitcast.10), calls=%async_computation.1 | async-start | bytes 327680 | tf_op jit(solution)/shard_map/all_to_all | solution.py:132
  40.4 0.1 broadcast_in_dim.37
  40.5 0.1 mul.53
  40.6 0.6 %copy-done.5 = f32[32]{0:T(128)S(1)} copy-done((f32[32]{0:T(128)S(1)}, f32[32]{0:T(128)}, u32[]{:S(2)}) %copy-start.5) | copy-done | bytes 152
  41.1 0.1 broadcast_in_dim.38
  41.2 0.1 mul.59
  41.3 7.3 %all-to-all-done.1 = bf16[8,16,544]{2,1,0:T(8,128)(2,1)S(1)} async-done(((bf16[8,16,544]{2,1,0:T(8,128)(2,1)}), bf16[8,16,544]{2,1,0:T(8,128)(2,1)S(1)}, u32[]{:S(2)}, u32[]{:S(2)}) %all-to-all-start.1) | async-done | bytes 139296 | tf_op jit(solution)/shard_map/all_to_all | solution.py:132
  48.6 0.0 copy-start.3
  48.7 0.7 %copy-done.3 = f32[512]{0:T(512)S(1)} copy-done((f32[512]{0:T(512)S(1)}, f32[512]{0:T(512)}, u32[]{:S(2)}) %copy-start.3) | copy-done | bytes 2072
  49.3 0.6 %fusion.7 = (f32[16,512]{1,0:T(8,128)S(1)}, f32[16,512]{1,0:T(8,128)}, f32[16,512]{1,0:T(8,128)}) fusion(f32[16,512]{1,0:T(8,128)S(1)} %copy-done.1, f32[512]{0:T(512)S(1)} %mul.59, f32[512]{0:T(512)S(1)} %copy-done.3, f32[512]{0:T(512)S(1)} %mul.53, f32[16,512]{1,0:T(8,128)S(1)} %copy-done.2, f32[16,544]{1,0:T(8,128)S(1)} %convert_reduce_fusion), kind=kLoop, calls=%fused_computation.23 | loop fusion | flops 81920 | bytes 202752 | tf_op jit(solution)/shard_map/mul | solution.py:140
  50.0 0.1 reshape.56
  50.1 0.1 fusion.12
  50.2 0.0 collective-permute-start.3
  50.2 0.5 collective-permute-start.4
  50.7 1.4 %collective-permute-start.5 = (f32[16,16]{1,0:T(8,128)S(1)}, f32[16,16]{1,0:T(8,128)S(1)}, u32[]{:S(2)}, u32[]{:S(2)}) collective-permute-start(f32[16,16]{1,0:T(8,128)S(1)} %fusion.12), channel_id=1, source_target_pairs={{0,3},{1,2},{2,1},{3,0},{4,7},{5,6},{6,5},{7,4},{8,11},{9,10},{10,... | collective-permute-start | bytes 3080 | tf_op jit(solution)/shard_map/ppermute | solution.py:26
  52.1 0.0 collective-permute-done.3
  52.1 1.9 %collective-permute-done.4 = f32[16,16]{1,0:T(8,128)S(1)} collective-permute-done((f32[16,16]{1,0:T(8,128)S(1)}, f32[16,16]{1,0:T(8,128)S(1)}, u32[]{:S(2)}, u32[]{:S(2)}) %collective-permute-start.4) | collective-permute-done | bytes 1056 | tf_op jit(solution)/shard_map/ppermute | solution.py:26
  53.9 0.0 collective-permute-done.5
  53.9 0.6 %add_add_fusion = f32[16,16]{1,0:T(8,128)} fusion(f32[16,16]{1,0:T(8,128)S(1)} %collective-permute-done.4, f32[16,16]{1,0:T(8,128)S(1)} %collective-permute-done.5, f32[16,16]{1,0:T(8,128)S(1)} %fusion.12, f32[16,16]{1,0:T(8,128)S(1)} %collective-permute-done.3), kind=kLoop, calls=%fused_computation.33 | loop fusion | flops 768 | bytes 5120 | tf_op jit(solution)/shard_map/add | solution.py:29
  (13 shorter events, 0.1 us)
Async XLA Ops:
  0.6 17.2 %copy-start = (bf16[128,32,128]{2,1,0:T(8,128)(2,1)S(1)}, bf16[128,32,128]{2,1,0:T(8,128)(2,1)}, u32[]{:S(2)}) copy-start(bf16[128,32,128]{2,1,0:T(8,128)(2,1)} %param.10) | copy-start | bytes 3145732
  2.4 14.7 %all-to-all-start = ((bf16[8,16,512]{2,1,0:T(8,128)(2,1)}), bf16[8,16,512]{2,1,0:T(8,128)(2,1)S(1)}, u32[]{:S(2)}, u32[]{:S(2)}) async-start(bf16[8,16,512]{2,1,0:T(8,128)(2,1)} %get-tuple-element.9), calls=%async_computation | async-start | bytes 262144 | tf_op jit(solution)/shard_map/all_to_all | solution.py:92
  9.7 0.7 %copy-start.7 = (s32[128]{0:T(128)S(1)}, s32[128]{0:T(128)}, u32[]{:S(2)}) copy-start(s32[128]{0:T(128)} %param.12) | copy-start | bytes 1540
  10.4 6.6 %copy-start.4 = (s32[128]{0:T(128)S(1)}, s32[128]{0:T(128)}, u32[]{:S(2)}) copy-start(s32[128]{0:T(128)} %param.13) | copy-start | bytes 1540
  18.3 5.2 %collective-permute-start = (bf16[32,16,128]{2,1,0:T(8,128)(2,1)S(1)}, bf16[32,16,128]{2,1,0:T(8,128)(2,1)S(1)}, u32[]{:S(2)}, u32[]{:S(2)}) collective-permute-start(bf16[32,16,128]{2,1,0:T(8,128)(2,1)S(1)} %get-tuple-element.17), channel_id=1, source_target_pairs={{0,1},{1,2},{2,3},{3,0},{4,5},{5,6},{6,7},{7,4},{8,9},{9,10},{10,1... | collective-permute-start | bytes 393224 | tf_op jit(solution)/shard_map/ppermute | solution.py:112
  18.4 6.4 %collective-permute-start.1 = (bf16[32,16,128]{2,1,0:T(8,128)(2,1)S(1)}, bf16[32,16,128]{2,1,0:T(8,128)(2,1)S(1)}, u32[]{:S(2)}, u32[]{:S(2)}) collective-permute-start(bf16[32,16,128]{2,1,0:T(8,128)(2,1)S(1)} %get-tuple-element.19), channel_id=1, source_target_pairs={{0,2},{1,3},{2,0},{3,1},{4,6},{5,7},{6,4},{7,5},{8,10},{9,11},{10,... | collective-permute-start | bytes 393224 | tf_op jit(solution)/shard_map/ppermute | solution.py:112
  20.0 6.0 %collective-permute-start.2 = (bf16[32,16,128]{2,1,0:T(8,128)(2,1)S(1)}, bf16[32,16,128]{2,1,0:T(8,128)(2,1)S(1)}, u32[]{:S(2)}, u32[]{:S(2)}) collective-permute-start(bf16[32,16,128]{2,1,0:T(8,128)(2,1)S(1)} %get-tuple-element.18), channel_id=1, source_target_pairs={{0,3},{1,0},{2,1},{3,2},{4,7},{5,4},{6,5},{7,6},{8,11},{9,8},{10,9... | collective-permute-start | bytes 393224 | tf_op jit(solution)/shard_map/ppermute | solution.py:112
  36.9 3.5 %copy-start.6 = (f32[32]{0:T(128)S(1)}, f32[32]{0:T(128)}, u32[]{:S(2)}) copy-start(f32[32]{0:T(128)} %param.18) | copy-start | bytes 388
  36.9 11.7 %all-to-all-start.1 = ((bf16[8,16,544]{2,1,0:T(8,128)(2,1)}), bf16[8,16,544]{2,1,0:T(8,128)(2,1)S(1)}, u32[]{:S(2)}, u32[]{:S(2)}) async-start(bf16[8,16,544]{2,1,0:T(8,128)(2,1)} %bitcast.10), calls=%async_computation.1 | async-start | bytes 327680 | tf_op jit(solution)/shard_map/all_to_all | solution.py:132
  40.5 0.7 %copy-start.5 = (f32[32]{0:T(128)S(1)}, f32[32]{0:T(128)}, u32[]{:S(2)}) copy-start(f32[32]{0:T(128)} %param.19) | copy-start | bytes 388
  41.3 7.4 %copy-start.1 = (f32[16,512]{1,0:T(8,128)S(1)}, f32[16,512]{1,0:T(8,128)}, u32[]{:S(2)}) copy-start(f32[16,512]{1,0:T(8,128)} %get-tuple-element.3) | copy-start | bytes 98308
  41.3 7.4 %copy-start.2 = (f32[16,512]{1,0:T(8,128)S(1)}, f32[16,512]{1,0:T(8,128)}, u32[]{:S(2)}) copy-start(f32[16,512]{1,0:T(8,128)} %get-tuple-element.8) | copy-start | bytes 98308
  48.6 0.7 %copy-start.3 = (f32[512]{0:T(512)S(1)}, f32[512]{0:T(512)}, u32[]{:S(2)}) copy-start(f32[512]{0:T(512)} %param.17) | copy-start | bytes 6148
  50.2 1.9 %collective-permute-start.3 = (f32[16,16]{1,0:T(8,128)S(1)}, f32[16,16]{1,0:T(8,128)S(1)}, u32[]{:S(2)}, u32[]{:S(2)}) collective-permute-start(f32[16,16]{1,0:T(8,128)S(1)} %fusion.12), channel_id=1, source_target_pairs={{0,1},{1,0},{2,3},{3,2},{4,5},{5,4},{6,7},{7,6},{8,9},{9,8},{10,11... | collective-permute-start | bytes 3080 | tf_op jit(solution)/shard_map/ppermute | solution.py:26
  50.2 3.7 %collective-permute-start.4 = (f32[16,16]{1,0:T(8,128)S(1)}, f32[16,16]{1,0:T(8,128)S(1)}, u32[]{:S(2)}, u32[]{:S(2)}) collective-permute-start(f32[16,16]{1,0:T(8,128)S(1)} %fusion.12), channel_id=1, source_target_pairs={{0,2},{1,3},{2,0},{3,1},{4,6},{5,7},{6,4},{7,5},{8,10},{9,11},{10,... | collective-permute-start | bytes 3080 | tf_op jit(solution)/shard_map/ppermute | solution.py:26
  50.7 3.2 %collective-permute-start.5 = (f32[16,16]{1,0:T(8,128)S(1)}, f32[16,16]{1,0:T(8,128)S(1)}, u32[]{:S(2)}, u32[]{:S(2)}) collective-permute-start(f32[16,16]{1,0:T(8,128)S(1)} %fusion.12), channel_id=1, source_target_pairs={{0,3},{1,2},{2,1},{3,0},{4,7},{5,6},{6,5},{7,4},{8,11},{9,10},{10,... | collective-permute-start | bytes 3080 | tf_op jit(solution)/shard_map/ppermute | solution.py:26

commit v5 on v4

--- a/solution.py
+++ b/solution.py
@@ -129,8 +129,22 @@
     low = (group_loglik - high.astype(jnp.float32)).astype(jnp.bfloat16)
     send = jnp.concatenate([group_grad, high, low], axis=1)
     send = send.reshape(owners, own_groups, block_width + 2 * chains)
-    got = lax.all_to_all(send, "dp", 0, 0, tiled=True)
-    summed = jnp.sum(got.astype(jnp.float32), axis=0)
+    if owners & (owners - 1) or owners > 2 * parts:
+        got = lax.all_to_all(send, "dp", 0, 0, tiled=True)
+        summed = jnp.sum(got.astype(jnp.float32), axis=0)
+    else:
+        me = lax.axis_index("dp")
+        halves = send.reshape(owners // 2, 2, own_groups, block_width + 2 * chains)
+        theirs = lax.dynamic_index_in_dim(halves, (me % 2) ^ 1, 1, False)
+        theirs = lax.ppermute(theirs, "dp", [(i, i ^ 1) for i in range(owners)])
+        kept = lax.dynamic_index_in_dim(halves, me % 2, 1, False).astype(jnp.float32)
+        kept = kept + theirs.astype(jnp.float32)
+        level = me // 2
+        summed = lax.dynamic_index_in_dim(kept, level, 0, False)
+        for k in range(1, owners // 2):
+            piece = lax.dynamic_index_in_dim(kept, level ^ k, 0, False)
+            piece = lax.ppermute(piece, "dp", [(i, i ^ (2 * k)) for i in range(owners)])
+            summed = summed + piece
     likelihood_grad = summed[:, :block_width]
     own_loglik = summed[:, block_width:block_width + chains] + summed[:, block_width + chains:]
 

time: 55 us -> 54.4 us (0.989)
  waiting for transfers between devices: 19.6 us -> 17.7 us
  starting transfers between devices: 15.7 us -> 16.9 us
  local copies, waits for them, and re-layouts: 3.84 us -> 4.52 us
  other arithmetic: 3.31 us -> 2.65 us
    all_to_all x1 -> x0, waiting for transfers between devices: 7.3 us -> none  [body(): got = lax.all_to_all(send, 'dp', 0, 0, tiled=True)]
    ppermute x0 -> x4, waiting for transfers between devices: none -> 5.47 us  [the longest x1 4.48 us: body(): theirs = lax.ppermute(theirs, 'dp', [(i, i ^ 1) for i in range(owners)])]
    ppermute x0 -> x4, starting transfers between devices: none -> 4.72 us  [the longest x3 4.44 us: body(): piece = lax.ppermute(piece, 'dp', [(i, i ^ 2 * k) for i in range(owners)])]
    all_to_all x1 -> x0, starting transfers between devices: 3.51 us -> none  [body(): got = lax.all_to_all(send, 'dp', 0, 0, tiled=True)]
    concatenate x1, other arithmetic: 0.76 us -> 0.09 us  [body(): send = jnp.concatenate([group_grad, high, low], axis=1)]
    unnamed x16, local copies, waits for them, and re-layouts: 1.91 us -> 2.56 us
  transfers between devices with their start and end apart: 8 -> 11, of which waited for: 6 -> 7; matrix products, arithmetic and copies ran while one was open for 2% -> 2% of each run, Pallas kernels for 0% -> 0%
where the time goes in v5:
time: 54.4 us; the launch traced here: 54 us
  waiting for transfers between devices  17.7 us (33%)
  starting transfers between devices  16.9 us (31%)
  blocking collectives  7.74 us (14%)
  local copies, waits for them, and re-layouts  4.52 us (8%)
  other arithmetic  2.65 us (5%)
  matrix products  1.88 us (3%)
  Pallas kernels  1.73 us (3%)
  between operations  0.84 us (2%)
    all_gather x1, blocking collectives, body(): all_residual = lax.all_gather(residual, 'feat', axis=0, tiled=True)  7.74 us
    all_to_all x1, starting transfers between devices, body(): lax.all_to_all(copies, 'dp', 0, 0, tiled=True).reshape(groups, block_width)  7.31 us
    all_to_all x1, waiting for transfers between devices, body(): lax.all_to_all(copies, 'dp', 0, 0, tiled=True).reshape(groups, block_width)  6.61 us
    ppermute x1, waiting for transfers between devices, body(): theirs = lax.ppermute(theirs, 'dp', [(i, i ^ 1) for i in range(owners)])  4.48 us
    ppermute x3, starting transfers between devices, body(): piece = lax.ppermute(piece, 'dp', [(i, i ^ 2 * k) for i in range(owners)])  4.44 us
    ppermute x3, waiting for transfers between devices, body(): lax.ppermute(piece, 'feat', [(i, (i + hop) % parts) for i in range(parts)])  3.79 us
    ppermute x3, starting transfers between devices, body(): lax.ppermute(piece, 'feat', [(i, (i + hop) % parts) for i in range(parts)])  3 us
    unnamed x16, local copies, waits for them, and re-layouts  2.56 us
  transfers between devices with their start and end apart: 11, of which 7 were waited for; matrix products, arithmetic and copies ran while one was open for 2% of the time, Pallas kernels for 0%

profile of v5, /device:TPU:0, one launch (start us, length us, event | category | flops | bytes accessed | tf_op | source)
XLA Modules:
  0.0 54.0 jit_solution(6465446434343333940)
XLA Ops:
  0.6 1.7 %opening.1 = (f32[16,512]{1,0:T(8,128)}, f32[16,512]{1,0:T(8,128)}, bf16[8,16,512]{2,1,0:T(8,128)(2,1)}) custom-call(f32[1,32]{1,0:T(1,128)} %bitcast.54, f32[16,512]{1,0:T(8,128)} %position_ref.1, f32[16,512]{1,0:T(8,128)} %momentum_ref.1, f32[16,512]{1,0:T(8,128)} %gradient_ref.1), custom_call_target="tpu_custom_call" | custom-call | tf_op jit(solution)/shard_map/opening/pallas_call | solution.py:55
  2.4 7.3 %all-to-all-start = ((bf16[8,16,512]{2,1,0:T(8,128)(2,1)}), bf16[8,16,512]{2,1,0:T(8,128)(2,1)S(1)}, u32[]{:S(2)}, u32[]{:S(2)}) async-start(bf16[8,16,512]{2,1,0:T(8,128)(2,1)} %get-tuple-element.9), calls=%async_computation | async-start | bytes 262144 | tf_op jit(solution)/shard_map/all_to_all | solution.py:92
  9.7 0.7 %copy-done.7 = s32[128]{0:T(128)S(1)} copy-done((s32[128]{0:T(128)S(1)}, s32[128]{0:T(128)}, u32[]{:S(2)}) %copy-start.7) | copy-done | bytes 536
  10.3 0.1 dynamic_slice.42
  10.4 6.6 %all-to-all-done = bf16[8,16,512]{2,1,0:T(8,128)(2,1)S(1)} async-done(((bf16[8,16,512]{2,1,0:T(8,128)(2,1)}), bf16[8,16,512]{2,1,0:T(8,128)(2,1)S(1)}, u32[]{:S(2)}, u32[]{:S(2)}) %all-to-all-start) | async-done | bytes 131104 | tf_op jit(solution)/shard_map/all_to_all | solution.py:92
  17.0 0.2 convolution_convert_fusion.2
  17.3 0.1 copy.30
  17.4 0.5 copy.31
  17.9 0.4 convolution_convert_fusion
  18.3 0.1 collective-permute-start
  18.4 1.6 %collective-permute-start.1 = (bf16[32,16,128]{2,1,0:T(8,128)(2,1)S(1)}, bf16[32,16,128]{2,1,0:T(8,128)(2,1)S(1)}, u32[]{:S(2)}, u32[]{:S(2)}) collective-permute-start(bf16[32,16,128]{2,1,0:T(8,128)(2,1)S(1)} %get-tuple-element.19), channel_id=1, source_target_pairs={{0,2},{1,3},{2,0},{3,1},{4,6},{5,7},{6,4},{7,5},{8,10},{9,11},{10,... | collective-permute-start | bytes 393224 | tf_op jit(solution)/shard_map/ppermute | solution.py:112
  20.0 1.4 %collective-permute-start.2 = (bf16[32,16,128]{2,1,0:T(8,128)(2,1)S(1)}, bf16[32,16,128]{2,1,0:T(8,128)(2,1)S(1)}, u32[]{:S(2)}, u32[]{:S(2)}) collective-permute-start(bf16[32,16,128]{2,1,0:T(8,128)(2,1)S(1)} %get-tuple-element.18), channel_id=1, source_target_pairs={{0,3},{1,0},{2,1},{3,2},{4,7},{5,4},{6,5},{7,6},{8,11},{9,8},{10,9... | collective-permute-start | bytes 393224 | tf_op jit(solution)/shard_map/ppermute | solution.py:112
  21.3 0.1 iota_compare_fusion.3
  21.4 0.1 dynamic_slice.48
  21.5 0.7 %dynamic-slice_convert_fusion = f32[32,128]{1,0:T(8,128)S(1)} fusion(s32[128,128]{1,0:T(8,128)} %param.11, s32[]{:T(128)S(6)} %select_n.74), kind=kLoop, calls=%fused_computation.35 | loop fusion | flops 4096 | bytes 32772 | tf_op jit(solution)/shard_map/convert_element_type | solution.py:13
  22.2 1.3 %collective-permute-done = bf16[32,16,128]{2,1,0:T(8,128)(2,1)S(1)} collective-permute-done((bf16[32,16,128]{2,1,0:T(8,128)(2,1)S(1)}, bf16[32,16,128]{2,1,0:T(8,128)(2,1)S(1)}, u32[]{:S(2)}, u32[]{:S(2)}) %collective-permute-start) | collective-permute-done | bytes 131104 | tf_op jit(solution)/shard_map/ppermute | solution.py:112
  23.5 1.3 %collective-permute-done.1 = bf16[32,16,128]{2,1,0:T(8,128)(2,1)S(1)} collective-permute-done((bf16[32,16,128]{2,1,0:T(8,128)(2,1)S(1)}, bf16[32,16,128]{2,1,0:T(8,128)(2,1)S(1)}, u32[]{:S(2)}, u32[]{:S(2)}) %collective-permute-start.1) | collective-permute-done | bytes 131104 | tf_op jit(solution)/shard_map/ppermute | solution.py:112
  24.8 1.2 %collective-permute-done.2 = bf16[32,16,128]{2,1,0:T(8,128)(2,1)S(1)} collective-permute-done((bf16[32,16,128]{2,1,0:T(8,128)(2,1)S(1)}, bf16[32,16,128]{2,1,0:T(8,128)(2,1)S(1)}, u32[]{:S(2)}, u32[]{:S(2)}) %collective-permute-start.2) | collective-permute-done | bytes 131104 | tf_op jit(solution)/shard_map/ppermute | solution.py:112
  26.0 0.4 select_convert_fusion
  26.4 7.7 %all_gather.3 = bf16[128,16,128]{2,1,0:T(8,128)(2,1)S(1)} all-gather(bf16[32,16,128]{2,1,0:T(8,128)(2,1)S(1)} %get-tuple-element.15), channel_id=1, replica_groups=mesh['dp'=8,'feat'=4] {'feat'}, dimensions={0}, use_global_device_ids=true | all-gather | bytes 655360 | tf_op jit(solution)/shard_map/all_gather | solution.py:115
  34.1 0.7 %convolution_bitcast_fusion = f32[128,32,16]{1,2,0:T(8,128)S(1)} fusion(bf16[128,16,128]{2,1,0:T(8,128)(2,1)S(1)} %all_gather.3, bf16[128,32,128]{2,1,0:T(8,128)(2,1)S(1)} %copy-done), kind=kOutput, calls=%fused_computation | convolution fusion | flops 16777216 | bytes 1835008 | tf_op jit(solution)/shard_map/tfr,tcr->tfc/dot_general | solution.py:116
  34.8 0.5 copy.32
  35.3 0.4 convolution_convert_fusion.1
  35.7 0.2 subtract_convert_fusion
  35.9 0.1 copy.33
  36.0 0.1 copy.34
  36.1 0.1 pad_maximum_fusion
  36.2 0.3 collective-permute-start.3
  36.5 4.5 %collective-permute-done.3 = bf16[4,16,544]{2,1,0:T(8,128)(2,1)S(1)} collective-permute-done((bf16[4,16,544]{2,1,0:T(8,128)(2,1)S(1)}, bf16[4,16,544]{2,1,0:T(8,128)(2,1)S(1)}, u32[]{:S(2)}, u32[]{:S(2)}) %collective-permute-start.3) | collective-permute-done | bytes 69664 | tf_op jit(solution)/shard_map/ppermute | solution.py:139
  41.1 0.1 collective-permute-start.4
  41.1 1.1 %collective-permute-start.5 = (f32[16,544]{1,0:T(8,128)S(1)}, f32[16,544]{1,0:T(8,128)S(1)}, u32[]{:S(2)}, u32[]{:S(2)}) collective-permute-start(f32[16,544]{1,0:T(8,128)S(1)} %get-tuple-element.22), channel_id=1, source_target_pairs={{0,16},{4,20},{8,24},{12,28},{16,0},{20,4},{24,8},{28,12},{1,17},{... | collective-permute-start | bytes 104456 | tf_op jit(solution)/shard_map/ppermute | solution.py:146
  42.2 3.3 %collective-permute-start.6 = (f32[16,544]{1,0:T(8,128)S(1)}, f32[16,544]{1,0:T(8,128)S(1)}, u32[]{:S(2)}, u32[]{:S(2)}) collective-permute-start(f32[16,544]{1,0:T(8,128)S(1)} %get-tuple-element.21), channel_id=1, source_target_pairs={{0,24},{4,28},{8,16},{12,20},{16,8},{20,12},{24,0},{28,4},{1,25},{... | collective-permute-start | bytes 104456 | tf_op jit(solution)/shard_map/ppermute | solution.py:146
  45.5 0.7 %copy-done.6 = f32[32]{0:T(128)S(1)} copy-done((f32[32]{0:T(128)S(1)}, f32[32]{0:T(128)}, u32[]{:S(2)}) %copy-start.6) | copy-done | bytes 152
  46.2 0.1 broadcast_in_dim.37
  46.2 0.1 mul.53
  46.3 0.6 %copy-done.5 = f32[32]{0:T(128)S(1)} copy-done((f32[32]{0:T(128)S(1)}, f32[32]{0:T(128)}, u32[]{:S(2)}) %copy-start.5) | copy-done | bytes 152
  46.9 0.1 broadcast_in_dim.38
  47.0 0.1 mul.59
  47.1 1.0 %collective-permute-done.6 = f32[16,544]{1,0:T(8,128)S(1)} collective-permute-done((f32[16,544]{1,0:T(8,128)S(1)}, f32[16,544]{1,0:T(8,128)S(1)}, u32[]{:S(2)}, u32[]{:S(2)}) %collective-permute-start.6) | collective-permute-done | bytes 34848 | tf_op jit(solution)/shard_map/ppermute | solution.py:146
  48.1 0.7 %copy-done.3 = f32[512]{0:T(512)S(1)} copy-done((f32[512]{0:T(512)S(1)}, f32[512]{0:T(512)}, u32[]{:S(2)}) %copy-start.3) | copy-done | bytes 2072
  48.8 0.6 %fusion.9 = (f32[16,512]{1,0:T(8,128)S(1)}, f32[16,512]{1,0:T(8,128)}, f32[16,512]{1,0:T(8,128)}) fusion(f32[16,512]{1,0:T(8,128)S(1)} %copy-done.1, f32[512]{0:T(512)S(1)} %mul.59, f32[512]{0:T(512)S(1)} %copy-done.3, f32[512]{0:T(512)S(1)} %mul.53, f32[16,512]{1,0:T(8,128)S(1)} %copy-done.2, f32[16,544]{1,0:T(8,128)S(1)} %fusion.7), kind=kLoop, calls=%fused_computation.30 | loop fusion | flops 81920 | bytes 202752 | tf_op jit(solution)/shard_map/mul | solution.py:154
  49.4 0.1 reshape.54
  49.6 0.1 fusion.14
  49.6 0.0 collective-permute-start.7
  49.7 0.5 collective-permute-start.8
  50.2 1.4 %collective-permute-start.9 = (f32[16,16]{1,0:T(8,128)S(1)}, f32[16,16]{1,0:T(8,128)S(1)}, u32[]{:S(2)}, u32[]{:S(2)}) collective-permute-start(f32[16,16]{1,0:T(8,128)S(1)} %fusion.14), channel_id=1, source_target_pairs={{0,3},{1,2},{2,1},{3,0},{4,7},{5,6},{6,5},{7,4},{8,11},{9,10},{10,... | collective-permute-start | bytes 3080 | tf_op jit(solution)/shard_map/ppermute | solution.py:26
  51.5 1.9 %collective-permute-done.8 = f32[16,16]{1,0:T(8,128)S(1)} collective-permute-done((f32[16,16]{1,0:T(8,128)S(1)}, f32[16,16]{1,0:T(8,128)S(1)}, u32[]{:S(2)}, u32[]{:S(2)}) %collective-permute-start.8) | collective-permute-done | bytes 1056 | tf_op jit(solution)/shard_map/ppermute | solution.py:26
  53.4 0.6 %add_add_fusion = f32[16,16]{1,0:T(8,128)} fusion(f32[16,16]{1,0:T(8,128)S(1)} %collective-permute-done.8, f32[16,16]{1,0:T(8,128)S(1)} %collective-permute-done.9, f32[16,16]{1,0:T(8,128)S(1)} %fusion.14, f32[16,16]{1,0:T(8,128)S(1)} %collective-permute-done.7), kind=kLoop, calls=%fused_computation.40 | loop fusion | flops 768 | bytes 5120 | tf_op jit(solution)/shard_map/add | solution.py:29
  (22 shorter events, 0.2 us)
Async XLA Ops:
  0.6 17.2 %copy-start = (bf16[128,32,128]{2,1,0:T(8,128)(2,1)S(1)}, bf16[128,32,128]{2,1,0:T(8,128)(2,1)}, u32[]{:S(2)}) copy-start(bf16[128,32,128]{2,1,0:T(8,128)(2,1)} %param.10) | copy-start | bytes 3145732
  2.4 14.7 %all-to-all-start = ((bf16[8,16,512]{2,1,0:T(8,128)(2,1)}), bf16[8,16,512]{2,1,0:T(8,128)(2,1)S(1)}, u32[]{:S(2)}, u32[]{:S(2)}) async-start(bf16[8,16,512]{2,1,0:T(8,128)(2,1)} %get-tuple-element.9), calls=%async_computation | async-start | bytes 262144 | tf_op jit(solution)/shard_map/all_to_all | solution.py:92
  9.7 0.7 %copy-start.7 = (s32[128]{0:T(128)S(1)}, s32[128]{0:T(128)}, u32[]{:S(2)}) copy-start(s32[128]{0:T(128)} %param.12) | copy-start | bytes 1540
  10.4 6.6 %copy-start.4 = (s32[128]{0:T(128)S(1)}, s32[128]{0:T(128)}, u32[]{:S(2)}) copy-start(s32[128]{0:T(128)} %param.13) | copy-start | bytes 1540
  18.3 5.2 %collective-permute-start = (bf16[32,16,128]{2,1,0:T(8,128)(2,1)S(1)}, bf16[32,16,128]{2,1,0:T(8,128)(2,1)S(1)}, u32[]{:S(2)}, u32[]{:S(2)}) collective-permute-start(bf16[32,16,128]{2,1,0:T(8,128)(2,1)S(1)} %get-tuple-element.17), channel_id=1, source_target_pairs={{0,1},{1,2},{2,3},{3,0},{4,5},{5,6},{6,7},{7,4},{8,9},{9,10},{10,1... | collective-permute-start | bytes 393224 | tf_op jit(solution)/shard_map/ppermute | solution.py:112
  18.4 6.4 %collective-permute-start.1 = (bf16[32,16,128]{2,1,0:T(8,128)(2,1)S(1)}, bf16[32,16,128]{2,1,0:T(8,128)(2,1)S(1)}, u32[]{:S(2)}, u32[]{:S(2)}) collective-permute-start(bf16[32,16,128]{2,1,0:T(8,128)(2,1)S(1)} %get-tuple-element.19), channel_id=1, source_target_pairs={{0,2},{1,3},{2,0},{3,1},{4,6},{5,7},{6,4},{7,5},{8,10},{9,11},{10,... | collective-permute-start | bytes 393224 | tf_op jit(solution)/shard_map/ppermute | solution.py:112
  20.0 6.0 %collective-permute-start.2 = (bf16[32,16,128]{2,1,0:T(8,128)(2,1)S(1)}, bf16[32,16,128]{2,1,0:T(8,128)(2,1)S(1)}, u32[]{:S(2)}, u32[]{:S(2)}) collective-permute-start(bf16[32,16,128]{2,1,0:T(8,128)(2,1)S(1)} %get-tuple-element.18), channel_id=1, source_target_pairs={{0,3},{1,0},{2,1},{3,2},{4,7},{5,4},{6,5},{7,6},{8,11},{9,8},{10,9... | collective-permute-start | bytes 393224 | tf_op jit(solution)/shard_map/ppermute | solution.py:112
  36.2 4.8 %collective-permute-start.3 = (bf16[4,16,544]{2,1,0:T(8,128)(2,1)S(1)}, bf16[4,16,544]{2,1,0:T(8,128)(2,1)S(1)}, u32[]{:S(2)}, u32[]{:S(2)}) collective-permute-start(bf16[4,16,544]{2,1,0:T(8,128)(2,1)S(1)} %dynamic-slice_bitcast_fusion.3), channel_id=1, source_target_pairs={{0,4},{4,0},{8,12},{12,8},{16,20},{20,16},{24,28},{28,24},{1,5},{5... | collective-permute-start | bytes 208904 | tf_op jit(solution)/shard_map/ppermute | solution.py:139
  41.1 6.0 %collective-permute-start.4 = (f32[16,544]{1,0:T(8,128)S(1)}, f32[16,544]{1,0:T(8,128)S(1)}, u32[]{:S(2)}, u32[]{:S(2)}) collective-permute-start(f32[16,544]{1,0:T(8,128)S(1)} %get-tuple-element.20), channel_id=1, source_target_pairs={{0,8},{4,12},{8,0},{12,4},{16,24},{20,28},{24,16},{28,20},{1,9},{5... | collective-permute-start | bytes 104456 | tf_op jit(solution)/shard_map/ppermute | solution.py:146
  41.1 5.9 %collective-permute-start.5 = (f32[16,544]{1,0:T(8,128)S(1)}, f32[16,544]{1,0:T(8,128)S(1)}, u32[]{:S(2)}, u32[]{:S(2)}) collective-permute-start(f32[16,544]{1,0:T(8,128)S(1)} %get-tuple-element.22), channel_id=1, source_target_pairs={{0,16},{4,20},{8,24},{12,28},{16,0},{20,4},{24,8},{28,12},{1,17},{... | collective-permute-start | bytes 104456 | tf_op jit(solution)/shard_map/ppermute | solution.py:146
  42.2 5.8 %collective-permute-start.6 = (f32[16,544]{1,0:T(8,128)S(1)}, f32[16,544]{1,0:T(8,128)S(1)}, u32[]{:S(2)}, u32[]{:S(2)}) collective-permute-start(f32[16,544]{1,0:T(8,128)S(1)} %get-tuple-element.21), channel_id=1, source_target_pairs={{0,24},{4,28},{8,16},{12,20},{16,8},{20,12},{24,0},{28,4},{1,25},{... | collective-permute-start | bytes 104456 | tf_op jit(solution)/shard_map/ppermute | solution.py:146
  45.5 0.7 %copy-start.6 = (f32[32]{0:T(128)S(1)}, f32[32]{0:T(128)}, u32[]{:S(2)}) copy-start(f32[32]{0:T(128)} %param.18) | copy-start | bytes 388
  46.2 0.7 %copy-start.5 = (f32[32]{0:T(128)S(1)}, f32[32]{0:T(128)}, u32[]{:S(2)}) copy-start(f32[32]{0:T(128)} %param.19) | copy-start | bytes 388
  47.0 1.0 %copy-start.1 = (f32[16,512]{1,0:T(8,128)S(1)}, f32[16,512]{1,0:T(8,128)}, u32[]{:S(2)}) copy-start(f32[16,512]{1,0:T(8,128)} %get-tuple-element.3) | copy-start | bytes 98308
  47.0 1.0 %copy-start.2 = (f32[16,512]{1,0:T(8,128)S(1)}, f32[16,512]{1,0:T(8,128)}, u32[]{:S(2)}) copy-start(f32[16,512]{1,0:T(8,128)} %get-tuple-element.8) | copy-start | bytes 98308
  48.1 0.7 %copy-start.3 = (f32[512]{0:T(512)S(1)}, f32[512]{0:T(512)}, u32[]{:S(2)}) copy-start(f32[512]{0:T(512)} %param.17) | copy-start | bytes 6148
  49.6 1.9 %collective-permute-start.7 = (f32[16,16]{1,0:T(8,128)S(1)}, f32[16,16]{1,0:T(8,128)S(1)}, u32[]{:S(2)}, u32[]{:S(2)}) collective-permute-start(f32[16,16]{1,0:T(8,128)S(1)} %fusion.14), channel_id=1, source_target_pairs={{0,1},{1,0},{2,3},{3,2},{4,5},{5,4},{6,7},{7,6},{8,9},{9,8},{10,11... | collective-permute-start | bytes 3080 | tf_op jit(solution)/shard_map/ppermute | solution.py:26
  49.7 3.7 %collective-permute-start.8 = (f32[16,16]{1,0:T(8,128)S(1)}, f32[16,16]{1,0:T(8,128)S(1)}, u32[]{:S(2)}, u32[]{:S(2)}) collective-permute-start(f32[16,16]{1,0:T(8,128)S(1)} %fusion.14), channel_id=1, source_target_pairs={{0,2},{1,3},{2,0},{3,1},{4,6},{5,7},{6,4},{7,5},{8,10},{9,11},{10,... | collective-permute-start | bytes 3080 | tf_op jit(solution)/shard_map/ppermute | solution.py:26
  50.2 3.2 %collective-permute-start.9 = (f32[16,16]{1,0:T(8,128)S(1)}, f32[16,16]{1,0:T(8,128)S(1)}, u32[]{:S(2)}, u32[]{:S(2)}) collective-permute-start(f32[16,16]{1,0:T(8,128)S(1)} %fusion.14), channel_id=1, source_target_pairs={{0,3},{1,2},{2,1},{3,0},{4,7},{5,6},{6,5},{7,4},{8,11},{9,10},{10,... | collective-permute-start | bytes 3080 | tf_op jit(solution)/shard_map/ppermute | solution.py:26
